TPU v7x, 32 devices: a whole 2x2x4 slice. The times are simulated.
32 devices in a mesh: ens: 2 (over x), tile: 16 (over z, y, core).
Axes of the slice: x: 2, y: 2, z: 4, core: 2. Of those that a mesh axis runs over, the one named last changes fastest.
Arguments:
- atmosphere: bfloat16 [256, 256, 128], P(('ens', 'tile')), parts along dimension 0, may hold values from -6 to 6
- ocean_state: bfloat16 [4096, 512], P(('ens', 'tile')), parts along dimension 0, may hold values from -6 to 6
- land_sea: int32 [2048], P('tile'), may hold values 0 or 1
- owners: int32 [2048, 1], P('tile'), may hold values from 0 to 15; in each aligned block of 128 rows (0 to 127, 128 to 255, ...) at most 16 rows name the same one
- rotations: int32 [16], replicated, may hold values from 0 to 255
- conv_weight: bfloat16 [3, 9, 128, 128], replicated, may hold values from -0.1875 to 0.1875
- conv_bias: bfloat16 [3, 128], replicated, may hold values from -3 to 3
- force_weight: bfloat16 [128, 32], replicated, may hold values from -0.5 to 0.5
- ocean_weight: bfloat16 [16, 9, 64, 32], P('tile'), may hold values from -0.25 to 0.25
Outputs:
- atmos_out: bfloat16 [256, 256, 128], P(('ens', 'tile')), parts along dimension 0
- sea_state: bfloat16 [4096, 512], P(('ens', 'tile')), parts along dimension 0
There are 2 independent parts, one for each index of `ens`. A program takes and returns all parts, laid end to end along the dimension named above; an argument that names none is the same for every part. Nothing has to cross between parts.
Inputs may be any that keep to these rules, and one draw needn't show every extreme that they name: `owners`: among the 128 blocks of one band no owner appears more than 16 times, and some owner appears exactly 16 times.
All inputs are finite; a program needn't handle non-finite values. No bound on the sum of `land_sea` on one device may be relied on, other than what follows from the above.
Results may differ from a plain program's by a relative error of at most 0.009.
Values may be sent and summed in bfloat16 or wider, within the bound.
No kernel may reach another device: no remote copies, remote signals or barrier semaphores. Data moves between devices by JAX's collectives and lax.ppermute only.
A program may use at most 64 MiB of HBM per device.

v0:
```python
import functools

import jax
import jax.numpy as jnp
from jax import lax
from jax.experimental import pallas as pl
from jax.experimental.pallas import tpu as pltpu
from jax.sharding import PartitionSpec as P

LEADS = 2
LAYERS = 3
BH = 4
BW = 4
SUB = 16
PAD = 4
MARGIN = 2**LAYERS - 1
F32 = jnp.float32
BF16 = jnp.bfloat16
VMEM = pltpu.MemorySpace.VMEM
SMEM = pltpu.MemorySpace.SMEM


def gelu(x):
    half = 0.5 * x
    inner = x * (0.7978845608028654 + 0.035677408136300125 * (x * x))
    return half + half * jnp.tanh(inner)


def one_hot_columns(columns, shift, source_permuted, target_permuted):
    target = lax.broadcasted_iota(jnp.int32, (columns, columns), 0)
    source = lax.broadcasted_iota(jnp.int32, (columns, columns), 1)
    tiles = columns // SUB
    if target_permuted:
        target = (target % SUB) * tiles + target // SUB
    if source_permuted:
        source = (source % SUB) * tiles + source // SUB
    wanted = (target + shift) & (columns - 1)
    return jnp.where(wanted == source, 1.0, 0.0).astype(BF16)


def store_row(buf, row, value, reach):
    columns = value.shape[0]
    buf[row, PAD * SUB : PAD * SUB + columns, :] = value.astype(BF16)
    for k in range(reach):
        first = value[k * SUB : (k + 1) * SUB]
        at = PAD * SUB + columns + k * SUB
        buf[row, at : at + SUB, :] = pltpu.roll(first, SUB - 1, 0).astype(BF16)
        low = columns - (k + 1) * SUB
        last = value[low : low + SUB]
        at = PAD * SUB - (k + 1) * SUB
        buf[row, at : at + SUB, :] = pltpu.roll(last, 1, 0).astype(BF16)


def place_rows(buf, source, first_row, count, hot, reach, columns, source_at=0):
    for k in range(0, count, 2):
        pair = source[source_at + k]
        if k + 1 < count:
            pair = jnp.concatenate([pair, source[source_at + k + 1]], axis=1)
        moved = jnp.dot(hot, pair, preferred_element_type=F32)
        store_row(buf, first_row + k, moved[:, :128], reach)
        if k + 1 < count:
            store_row(buf, first_row + k + 1, moved[:, 128:], reach)


def conv_layer(src, dst, weights, bias, layer, groups, reach, inside, columns):
    dilation = 2**layer
    offset = bias[layer][None, :].astype(F32)

    def pair_at(row):
        pieces = []
        for rho in range(4):
            for tap in range(3):
                start = (PAD + (tap - 1) * dilation) * SUB
                pieces.append(src[row + (rho - 1) * dilation, start : start + columns, :])
        summed = jnp.dot(
            jnp.concatenate(pieces, axis=1), weights[layer], preferred_element_type=F32
        )
        for half in range(2):
            at = row + half * dilation
            kept = src[at, PAD * SUB : PAD * SUB + columns, :].astype(F32)
            value = kept + gelu(summed[:, half * 128 : half * 128 + 128] + offset)
            if inside is not None:
                value = value * inside(at)
            store_row(dst, at, value, reach)

    for first, step, count in groups:

        def body(k, carry, first=first, step=step):
            pair_at(first + k * step)
            return carry

        lax.fori_loop(0, count, body, 0)


def lead_rows(buf_a, buf_b, weights, bias, info, band_rows, columns):
    low = info[2].astype(F32)
    high = info[3].astype(F32)

    def inside(row):
        return jnp.where(row < MARGIN, low, jnp.where(row >= MARGIN + band_rows, high, 1.0))

    conv_layer(buf_a, buf_b, weights, bias, 0, [(1, 2, 10)], 2, inside, columns)
    conv_layer(buf_b, buf_a, weights, bias, 1, [(3, 4, 4), (4, 4, 4)], 4, inside, columns)
    conv_layer(buf_a, buf_b, weights, bias, 2, [(MARGIN, 1, 4)], 0, None, columns)


def prep_kernel(own, conv_weight, field, weights):
    columns = own.shape[1]
    hot = one_hot_columns(columns, 0, False, True)
    place_rows(field, own, 0, own.shape[0], hot, 1, columns)
    weights[...] = jnp.zeros_like(weights)
    for layer in range(LAYERS):
        for tap_row in range(3):
            for tap in range(3):
                tile = conv_weight[layer, tap_row * 3 + tap]
                for half in range(2):
                    at = ((tap_row + half) * 3 + tap) * 128
                    weights[layer, at : at + 128, half * 128 : half * 128 + 128] = tile


def lead_one_kernel(info, own, up, down, weights, bias, field, send_up, send_down, buf_a, buf_b):
    band_rows, columns = own.shape[0], up.shape[1]
    buf_a[MARGIN : MARGIN + band_rows] = own[...]
    hot = one_hot_columns(columns, info[0], False, True)
    place_rows(buf_a, up, 0, MARGIN, hot, 1, columns)
    hot = one_hot_columns(columns, info[1], False, True)
    place_rows(buf_a, down, MARGIN + band_rows, MARGIN, hot, 1, columns)
    lead_rows(buf_a, buf_b, weights, bias, info, band_rows, columns)
    for row in range(band_rows):
        value = buf_b[MARGIN + row, PAD * SUB : PAD * SUB + columns, :]
        store_row(field, row, value.astype(F32), 1)
        if row < MARGIN:
            send_down[row] = value
        if row >= band_rows - MARGIN:
            send_up[row - (band_rows - MARGIN)] = value


def table_kernel(gathered, table):
    lanes_from = lax.broadcasted_iota(jnp.int32, (128, 512), 0)
    lanes_to = lax.broadcasted_iota(jnp.int32, (128, 512), 1)
    cell = lanes_to // 128
    spread = jnp.where(lanes_to % 128 - lanes_from == 32 * (cell - 1), 1.0, 0.0).astype(BF16)

    def body(owner, carry):
        for tap_row in range(3):
            wide = jnp.dot(gathered[owner, tap_row], spread, preferred_element_type=F32)
            for half in range(2):
                for q in range(4):
                    at = tap_row * 256 + half * 128 + q * 32
                    table[owner, at : at + 32, :] = wide[
                        half * 32 : half * 32 + 32, q * 128 : q * 128 + 128
                    ].astype(BF16)
        return carry

    lax.fori_loop(0, gathered.shape[0], body, 0)


def block_lanes(channel_major_rows):
    a = lax.broadcasted_iota(jnp.int32, (512, 512), 0)
    b = lax.broadcasted_iota(jnp.int32, (512, 512), 1)
    src, dst = (a, b) if channel_major_rows else (b, a)
    wanted = (dst % 32) * 16 + dst // 32
    return jnp.where(src == wanted, 1.0, 0.0).astype(BF16)


def lead_two_kernel(
    info, own, up, down, weights, bias, force, table, state, owners, sea,
    atmos_out, sea_state, buf_a, buf_b, joined, acc,
):
    band_rows, columns = own.shape[0], up.shape[1]
    buf_a[MARGIN : MARGIN + band_rows] = own[...]
    hot = one_hot_columns(columns, info[0], True, True)
    place_rows(buf_a, up, 0, MARGIN, hot, 1, columns)
    hot = one_hot_columns(columns, info[1], True, True)
    place_rows(buf_a, down, MARGIN + band_rows, MARGIN, hot, 1, columns)
    lead_rows(buf_a, buf_b, weights, bias, info, band_rows, columns)
    hot = one_hot_columns(columns, 0, True, False)
    for row in range(0, band_rows, 2):
        pair = [
            buf_b[MARGIN + row + k, PAD * SUB : PAD * SUB + columns, :] for k in range(2)
        ]
        moved = jnp.dot(hot, jnp.concatenate(pair, axis=1), preferred_element_type=F32)
        atmos_out[row] = moved[:, :128].astype(BF16)
        atmos_out[row + 1] = moved[:, 128:].astype(BF16)

    blocks = band_rows // BH * (columns // BW)
    per_half = columns // BW
    wide = force[...]
    zero = jnp.zeros((128, 32), BF16)
    spread = jnp.concatenate(
        [
            jnp.concatenate([wide if q == p else zero for p in range(4)], axis=1)
            for q in range(4)
        ],
        axis=0,
    )
    spread = jnp.concatenate([spread, spread], axis=0)
    forcing = []
    for i in range(BH):
        pieces = []
        for half in range(band_rows // BH):
            row = half * BH + i
            for g in range(SUB // BW):
                cells = []
                for field, at in ((own, row), (buf_b, MARGIN + row)):
                    for q in range(BW):
                        tile = (PAD + g * BW + q) * SUB
                        cells.append(field[at, tile : tile + SUB, :])
                pieces.append(jnp.concatenate(cells, axis=1))
        wide = jnp.concatenate(pieces, axis=0)
        forcing.append(
            (0.5 * jnp.dot(wide, spread, preferred_element_type=F32)).astype(BF16)
        )
    forcing = jnp.concatenate(forcing, axis=1)
    a = lax.broadcasted_iota(jnp.int32, (blocks, blocks), 0)
    b = lax.broadcasted_iota(jnp.int32, (blocks, blocks), 1)
    source = (a // per_half) * per_half + (a % 4) * SUB + (a % per_half) // 4
    order = jnp.where(source == b, 1.0, 0.0).astype(BF16)
    forcing = jnp.dot(order, forcing, preferred_element_type=F32).astype(BF16)
    own_state = jnp.dot(
        state[...], block_lanes(True), preferred_element_type=F32
    ).astype(BF16)
    joined[...] = jnp.zeros_like(joined)
    for i in range(BH):
        for tap_row in range(3):
            at = i + tap_row - 1
            if 0 <= at < BH:
                here = pl.ds(i * blocks, blocks)
                joined[here, tap_row * 256 : tap_row * 256 + 128] = forcing[
                    :, at * 128 : at * 128 + 128
                ]
                joined[here, tap_row * 256 + 128 : tap_row * 256 + 256] = own_state[
                    :, at * 128 : at * 128 + 128
                ]
    owner = jnp.broadcast_to(owners[...], (blocks, 128))

    def body(k, carry):
        pair = jnp.concatenate([table[2 * k], table[2 * k + 1]], axis=1)
        for i in range(BH):
            here = pl.ds(i * blocks, blocks)
            got = jnp.dot(joined[here, :], pair, preferred_element_type=F32)
            old = acc[here, :]
            new = jnp.where(owner == 2 * k, got[:, :128], old)
            acc[here, :] = jnp.where(owner == 2 * k + 1, got[:, 128:], new)
        return carry

    acc[...] = jnp.zeros_like(acc)
    lax.fori_loop(0, table.shape[0] // 2, body, 0)
    fresh = []
    for i in range(BH):
        kept = own_state[:, i * 128 : i * 128 + 128].astype(F32)
        fresh.append((kept + gelu(acc[i * blocks : (i + 1) * blocks, :])).astype(BF16))
    result = jnp.dot(
        jnp.concatenate(fresh, axis=1), block_lanes(False), preferred_element_type=F32
    )
    flag = jnp.broadcast_to(sea[...], (blocks, 512))
    sea_state[...] = jnp.where(flag > 0, result, 0.0).astype(BF16)


def call(kernel, out_shape, scratch, specs, name):
    return pl.pallas_call(
        kernel,
        out_shape=out_shape,
        in_specs=[pl.BlockSpec(memory_space=s) for s in specs],
        out_specs=jax.tree.map(lambda _: pl.BlockSpec(memory_space=VMEM), out_shape),
        scratch_shapes=scratch,
        name=name,
        compiler_params=pltpu.CompilerParams(vmem_limit_bytes=56 * 2**20),
    )


def local(
    atmosphere, ocean_state, land_sea, owners, rotations,
    conv_weight, conv_bias, force_weight, ocean_weight,
):
    tile = lax.axis_index("tile")
    tiles = lax.axis_size("tile")
    band_rows, columns, channels = atmosphere.shape
    blocks = owners.shape[0]
    shape = jax.ShapeDtypeStruct
    up_pairs = [(i, i + 1) for i in range(tiles - 1)]
    down_pairs = [(j, i) for i, j in up_pairs]

    own_shift = rotations[tile]
    up_shift = own_shift - rotations[jnp.maximum(tile - 1, 0)]
    down_shift = own_shift - rotations[jnp.minimum(tile + 1, tiles - 1)]
    info = jnp.stack(
        [up_shift, down_shift, (tile > 0).astype(jnp.int32), (tile < tiles - 1).astype(jnp.int32)]
    ).astype(jnp.int32)

    up = lax.ppermute(atmosphere[band_rows - MARGIN :], "tile", up_pairs)
    down = lax.ppermute(atmosphere[:MARGIN], "tile", down_pairs)

    taps = ocean_weight[0].reshape(3, 3, 64, 32)
    strip = jnp.concatenate(
        [taps[:, 2], taps[:, 1], taps[:, 0], jnp.zeros_like(taps[:, 0])], axis=-1
    )
    gathered = lax.all_to_all(
        jnp.broadcast_to(strip[None], (tiles, 3, 64, 128)), "tile", 0, 0, tiled=True
    )

    padded = columns + 2 * PAD * SUB
    field_shape = shape((band_rows, padded, channels), BF16)
    own, weights = call(
        prep_kernel,
        (field_shape, shape((LAYERS, 1536, 256), BF16)),
        [], [VMEM] * 2, "prep",
    )(atmosphere, conv_weight)

    buffers = [pltpu.VMEM((band_rows + 2 * MARGIN, padded, channels), BF16)] * 2
    halo = shape((MARGIN, columns, channels), BF16)
    lead_one, send_up, send_down = call(
        lead_one_kernel, (field_shape, halo, halo), buffers, [SMEM] + [VMEM] * 5, "lead_one"
    )(info, own, up, down, weights, conv_bias)

    up = lax.ppermute(send_up, "tile", up_pairs)
    down = lax.ppermute(send_down, "tile", down_pairs)

    table = call(
        table_kernel, shape((tiles, 768, 128), BF16), [], [VMEM], "table"
    )(gathered)

    return call(
        lead_two_kernel,
        (shape(atmosphere.shape, BF16), shape(ocean_state.shape, BF16)),
        buffers
        + [pltpu.VMEM((BH * blocks, 768), BF16), pltpu.VMEM((BH * blocks, 128), F32)],
        [SMEM] + [VMEM] * 10, "lead_two",
    )(
        info, lead_one, up, down, weights, conv_bias, force_weight, table,
        ocean_state, owners, land_sea[:, None],
    )


def solution(mesh):
    in_specs = (
        P(("ens", "tile"), None, None),
        P(("ens", "tile"), None),
        P("tile"),
        P("tile", None),
        P(),
        P(),
        P(),
        P(),
        P("tile", None, None, None),
    )
    out_specs = (P(("ens", "tile"), None, None), P(("ens", "tile"), None))
    return jax.shard_map(local, mesh=mesh, in_specs=in_specs, out_specs=out_specs, check_vma=False)
```

profile of v0, /device:TPU:16, one launch (start us, length us, event | category | flops | bytes accessed | tf_op | source)
XLA Modules:
  0.0 83.0 jit_solution(396168663344011584)
XLA Ops:
  0.6 0.0 copy-start
  0.7 0.8 %fusion.1 = (bf16[3,1,64,32]{2,3,1,0:T(8,128)(2,1)S(1)}, bf16[3,1,64,32]{2,3,1,0:T(8,128)(2,1)S(1)}, bf16[3,1,64,32]{2,3,1,0:T(8,128)(2,1)S(1)}) fusion(bf16[3,3,64,32]{2,3,1,0:T(8,128)(2,1)} %bitcast.10), kind=kLoop, calls=%fused_computation.3 | loop fusion | bytes 73728 | tf_op jit(solution)/shard_map/slice | solution.py:296
  1.5 0.1 copy.17
  1.6 0.1 copy.18
  1.7 0.1 copy.19
  1.8 0.1 pad.3.clone
  1.9 0.1 maximum_maximum_fusion
  2.0 1.1 %broadcast_in_dim.13 = bf16[16,3,64,128]{3,2,1,0:T(8,128)(2,1)} broadcast(bf16[3,64,128]{2,1,0:T(8,128)(2,1)S(1)} %maximum_maximum_fusion), dimensions={1,2,3} | broadcast | bytes 835584 | tf_op jit(solution)/shard_map/broadcast_in_dim | solution.py:299
  3.1 6.2 %all-to-all-start = ((bf16[16,3,64,128]{3,2,1,0:T(8,128)(2,1)}), bf16[16,3,64,128]{3,2,1,0:T(8,128)(2,1)S(1)}, u32[]{:S(2)}, u32[]{:S(2)}) async-start(bf16[16,3,64,128]{3,2,1,0:T(8,128)(2,1)} %broadcast_in_dim.13), calls=%async_computation | async-start | bytes 1572864 | tf_op jit(solution)/shard_map/all_to_all | solution.py:298
  9.3 0.2 fusion
  9.4 0.0 copy-start.8
  9.4 0.0 copy-start.9
  9.5 0.0 copy-start.6
  9.5 2.2 %collective-permute-start = (bf16[7,256,128]{2,1,0:T(8,128)(2,1)S(1)}, bf16[7,256,128]{2,1,0:T(8,128)(2,1)S(1)}, u32[]{:S(2)}, u32[]{:S(2)}) collective-permute-start(bf16[7,256,128]{2,1,0:T(8,128)(2,1)S(1)} %get-tuple-element.13), channel_id=1, source_target_pairs={{0,1},{1,2},{2,3},{3,4},{4,5},{5,6},{6,7},{7,8},{8,9},{9,10},{10,1... | collective-permute-start | bytes 1376264 | tf_op jit(solution)/shard_map/ppermute | solution.py:291
  11.6 4.4 %collective-permute-start.1 = (bf16[7,256,128]{2,1,0:T(8,128)(2,1)S(1)}, bf16[7,256,128]{2,1,0:T(8,128)(2,1)S(1)}, u32[]{:S(2)}, u32[]{:S(2)}) collective-permute-start(bf16[7,256,128]{2,1,0:T(8,128)(2,1)S(1)} %get-tuple-element.12), channel_id=1, source_target_pairs={{1,0},{2,1},{3,2},{4,3},{5,4},{6,5},{7,6},{8,7},{9,8},{10,9},{11,1... | collective-permute-start | bytes 1376264 | tf_op jit(solution)/shard_map/ppermute | solution.py:292
  16.1 0.7 fusion.2
  19.4 3.6 %prep.1 = (bf16[8,384,128]{2,1,0:T(8,128)(2,1)}, bf16[3,1536,256]{2,1,0:T(8,128)(2,1)}) custom-call(bf16[8,256,128]{2,1,0:T(8,128)(2,1)} %own.1, bf16[3,9,128,128]{3,2,1,0:T(8,128)(2,1)} %conv_weight.1), custom_call_target="tpu_custom_call" | custom-call | tf_op jit(solution)/shard_map/prep/pallas_call | solution.py:304
  23.0 0.6 pad_add_fusion.info
  23.6 10.2 %collective-permute-done.up = bf16[7,256,128]{2,1,0:T(8,128)(2,1)S(1)} collective-permute-done((bf16[7,256,128]{2,1,0:T(8,128)(2,1)S(1)}, bf16[7,256,128]{2,1,0:T(8,128)(2,1)S(1)}, u32[]{:S(2)}, u32[]{:S(2)}) %collective-permute-start) | collective-permute-done | bytes 458784 | tf_op jit(solution)/shard_map/ppermute | solution.py:291
  33.8 0.8 copy-done.2
  34.5 0.2 copy-done.3
  34.7 13.5 %lead_one.1 = (bf16[8,384,128]{2,1,0:T(8,128)(2,1)}, bf16[7,256,128]{2,1,0:T(8,128)(2,1)}, bf16[7,256,128]{2,1,0:T(8,128)(2,1)}) custom-call(s32[4]{0:T(128)} %pad_add_fusion.info, bf16[8,384,128]{2,1,0:T(8,128)(2,1)} %get-tuple-element.7.own, bf16[7,256,128]{2,1,0:T(8,128)(2,1)} %copy-done.2, bf16[7,256,128]{2,1,0:T(8,128)(2,1)} %copy-done.3, ...), custom_call_target="tpu_custom_call" | custom-call | tf_op jit(solution)/shard_map/lead_one/pallas_call | solution.py:312
  48.2 1.9 %collective-permute-start.2 = (bf16[7,256,128]{2,1,0:T(8,128)(2,1)}, bf16[7,256,128]{2,1,0:T(8,128)(2,1)S(1)}, u32[]{:S(2)}, u32[]{:S(2)}) collective-permute-start(bf16[7,256,128]{2,1,0:T(8,128)(2,1)} %get-tuple-element.10), channel_id=1, source_target_pairs={{0,1},{1,2},{2,3},{3,4},{4,5},{5,6},{6,7},{7,8},{8,9},{9,10},{10,1... | collective-permute-start | bytes 1376264 | tf_op jit(solution)/shard_map/ppermute | solution.py:316
  50.2 4.5 %collective-permute-start.3 = (bf16[7,256,128]{2,1,0:T(8,128)(2,1)}, bf16[7,256,128]{2,1,0:T(8,128)(2,1)S(1)}, u32[]{:S(2)}, u32[]{:S(2)}) collective-permute-start(bf16[7,256,128]{2,1,0:T(8,128)(2,1)} %get-tuple-element.11), channel_id=1, source_target_pairs={{1,0},{2,1},{3,2},{4,3},{5,4},{6,5},{7,6},{8,7},{9,8},{10,9},{11,1... | collective-permute-start | bytes 1376264 | tf_op jit(solution)/shard_map/ppermute | solution.py:317
  54.7 0.7 copy.15.owners
  55.5 0.7 copy.16.sea
  56.2 0.7 copy.14.force
  56.9 0.9 %copy-done.1 = bf16[16,3,64,128]{3,2,1,0:T(8,128)(2,1)} copy-done((bf16[16,3,64,128]{3,2,1,0:T(8,128)(2,1)}, bf16[16,3,64,128]{3,2,1,0:T(8,128)(2,1)S(1)}, u32[]{:S(2)}) %copy-start.1) | copy-done | bytes 786456
  57.8 6.1 %table.1 = bf16[16,768,128]{2,1,0:T(8,128)(2,1)} custom-call(bf16[16,3,64,128]{3,2,1,0:T(8,128)(2,1)} %copy-done.1), custom_call_target="tpu_custom_call" | custom-call | tf_op jit(solution)/shard_map/table/pallas_call | solution.py:319
  63.9 0.8 copy-done.4
  64.7 0.2 copy-done.5
  64.9 18.1 %lead_two.1 = (bf16[8,256,128]{2,1,0:T(8,128)(2,1)}, bf16[128,512]{1,0:T(8,128)(2,1)}) custom-call(s32[4]{0:T(128)} %pad_add_fusion.info, bf16[8,384,128]{2,1,0:T(8,128)(2,1)} %get-tuple-element.9.own, bf16[7,256,128]{2,1,0:T(8,128)(2,1)} %copy-done.4, bf16[7,256,128]{2,1,0:T(8,128)(2,1)} %copy-done.5, bf16[3,1536,256]{2,1,0:T(8,128)(2,1)} %get-tuple-element.8.weights, ...), custom_call_target="tpu_custom_call" | custom-call | tf_op jit(solution)/shard_map/lead_two/pallas_call | solution.py:323
  (16 shorter events, 0.0 us)
Async XLA Ops:
  0.6 8.6 %copy-start = (bf16[8,256,128]{2,1,0:T(8,128)(2,1)S(1)}, bf16[8,256,128]{2,1,0:T(8,128)(2,1)}, u32[]{:S(2)}) copy-start(bf16[8,256,128]{2,1,0:T(8,128)(2,1)} %own.1) | copy-start | bytes 1572868
  0.6 15.4 %copy-start.7 = (s32[16]{0:T(128)S(1)}, s32[16]{0:T(128)}, u32[]{:S(2)}) copy-start(s32[16]{0:T(128)} %param.13) | copy-start | bytes 196
  3.1 53.9 %all-to-all-start = ((bf16[16,3,64,128]{3,2,1,0:T(8,128)(2,1)}), bf16[16,3,64,128]{3,2,1,0:T(8,128)(2,1)S(1)}, u32[]{:S(2)}, u32[]{:S(2)}) async-start(bf16[16,3,64,128]{3,2,1,0:T(8,128)(2,1)} %broadcast_in_dim.13), calls=%async_computation | async-start | bytes 1572864 | tf_op jit(solution)/shard_map/all_to_all | solution.py:298
  9.4 45.3 %copy-start.8 = (s32[128,1]{0,1:T(1,128)S(1)}, s32[128,1]{0,1:T(1,128)}, u32[]{:S(2)}) copy-start(s32[128,1]{0,1:T(1,128)} %param.12) | copy-start | bytes 1540
  9.4 46.0 %copy-start.9 = (s32[128]{0:T(128)S(1)}, s32[128]{0:T(128)}, u32[]{:S(2)}) copy-start(s32[128]{0:T(128)} %param.11) | copy-start | bytes 1540
  9.5 46.8 %copy-start.6 = (bf16[128,32]{0,1:T(8,128)(2,1)S(1)}, bf16[128,32]{0,1:T(8,128)(2,1)}, u32[]{:S(2)}) copy-start(bf16[128,32]{0,1:T(8,128)(2,1)} %param.16) | copy-start | bytes 24580
  9.5 24.3 %collective-permute-start = (bf16[7,256,128]{2,1,0:T(8,128)(2,1)S(1)}, bf16[7,256,128]{2,1,0:T(8,128)(2,1)S(1)}, u32[]{:S(2)}, u32[]{:S(2)}) collective-permute-start(bf16[7,256,128]{2,1,0:T(8,128)(2,1)S(1)} %get-tuple-element.13), channel_id=1, source_target_pairs={{0,1},{1,2},{2,3},{3,4},{4,5},{5,6},{6,7},{7,8},{8,9},{9,10},{10,1... | collective-permute-start | bytes 1376264 | tf_op jit(solution)/shard_map/ppermute | solution.py:291
  11.6 22.2 %collective-permute-start.1 = (bf16[7,256,128]{2,1,0:T(8,128)(2,1)S(1)}, bf16[7,256,128]{2,1,0:T(8,128)(2,1)S(1)}, u32[]{:S(2)}, u32[]{:S(2)}) collective-permute-start(bf16[7,256,128]{2,1,0:T(8,128)(2,1)S(1)} %get-tuple-element.12), channel_id=1, source_target_pairs={{1,0},{2,1},{3,2},{4,3},{5,4},{6,5},{7,6},{8,7},{9,8},{10,9},{11,1... | collective-permute-start | bytes 1376264 | tf_op jit(solution)/shard_map/ppermute | solution.py:292
  33.8 0.8 copy-start.2
  33.8 0.9 %copy-start.3 = (bf16[7,256,128]{2,1,0:T(8,128)(2,1)}, bf16[7,256,128]{2,1,0:T(8,128)(2,1)S(1)}, u32[]{:S(2)}) copy-start(bf16[7,256,128]{2,1,0:T(8,128)(2,1)S(1)} %collective-permute-done.1.down) | copy-start | bytes 1376260
  48.2 15.7 %collective-permute-start.2 = (bf16[7,256,128]{2,1,0:T(8,128)(2,1)}, bf16[7,256,128]{2,1,0:T(8,128)(2,1)S(1)}, u32[]{:S(2)}, u32[]{:S(2)}) collective-permute-start(bf16[7,256,128]{2,1,0:T(8,128)(2,1)} %get-tuple-element.10), channel_id=1, source_target_pairs={{0,1},{1,2},{2,3},{3,4},{4,5},{5,6},{6,7},{7,8},{8,9},{9,10},{10,1... | collective-permute-start | bytes 1376264 | tf_op jit(solution)/shard_map/ppermute | solution.py:316
  50.2 13.8 %collective-permute-start.3 = (bf16[7,256,128]{2,1,0:T(8,128)(2,1)}, bf16[7,256,128]{2,1,0:T(8,128)(2,1)S(1)}, u32[]{:S(2)}, u32[]{:S(2)}) collective-permute-start(bf16[7,256,128]{2,1,0:T(8,128)(2,1)} %get-tuple-element.11), channel_id=1, source_target_pairs={{1,0},{2,1},{3,2},{4,3},{5,4},{6,5},{7,6},{8,7},{9,8},{10,9},{11,1... | collective-permute-start | bytes 1376264 | tf_op jit(solution)/shard_map/ppermute | solution.py:317
  56.9 0.9 %copy-start.1 = (bf16[16,3,64,128]{3,2,1,0:T(8,128)(2,1)}, bf16[16,3,64,128]{3,2,1,0:T(8,128)(2,1)S(1)}, u32[]{:S(2)}) copy-start(bf16[16,3,64,128]{3,2,1,0:T(8,128)(2,1)S(1)} %all-to-all-done.gathered) | copy-start | bytes 2359300
  63.9 0.8 copy-start.4
  63.9 0.9 %copy-start.5 = (bf16[7,256,128]{2,1,0:T(8,128)(2,1)}, bf16[7,256,128]{2,1,0:T(8,128)(2,1)S(1)}, u32[]{:S(2)}) copy-start(bf16[7,256,128]{2,1,0:T(8,128)(2,1)S(1)} %collective-permute-done.3.down) | copy-start | bytes 1376260
where the time goes:
time: 83.4 us; the launch traced here: 83 us
  Pallas kernels  41.4 us (50%)
  starting transfers between devices  19.2 us (23%)
  waiting for transfers between devices  10.2 us (12%)
  local copies, waits for them, and re-layouts  8.12 us (10%)
  between operations  3.41 us (4%)
    pallas_call x1, Pallas kernels, local(): call(lead_two_kernel, (shape(atmosphere.shape, BF16), shape(ocean_state.s...  18.1 us
    pallas_call x1, Pallas kernels, local(): call(lead_one_kernel, (field_shape, halo, halo), buffers, [SMEM] + [VMEM]...  13.5 us
    ppermute x1, waiting for transfers between devices, local(): up = lax.ppermute(atmosphere[band_rows - MARGIN:], 'tile', up_pairs)  10.2 us
    all_to_all x1, starting transfers between devices, local(): lax.all_to_all(jnp.broadcast_to(strip[None], (tiles, 3, 64, 128)), 'tile'...  6.18 us
    pallas_call x1, Pallas kernels, local(): call(table_kernel, shape((tiles, 768, 128), BF16), [], [VMEM], 'table')  6.07 us
    unnamed x25, local copies, waits for them, and re-layouts  4.57 us
    ppermute x1, starting transfers between devices, local(): down = lax.ppermute(send_down, 'tile', down_pairs)  4.54 us
    ppermute x1, starting transfers between devices, local(): down = lax.ppermute(atmosphere[:MARGIN], 'tile', down_pairs)  4.44 us
  transfers between devices with their start and end apart: 5, of which 1 were waited for; matrix products, arithmetic and copies ran while one was open for 4% of the time, Pallas kernels for 28%

commit v1 on v0

v1 whole, which is shorter than its diff:
```python
import jax
import jax.numpy as jnp
from jax import lax
from jax.experimental import pallas as pl
from jax.experimental.pallas import tpu as pltpu
from jax.sharding import PartitionSpec as P


LAYERS = 3
BH = 4
BW = 4
SUB = 16
PAD = 4
GROUP = 2
MARGIN = 2**LAYERS - 1
F32 = jnp.float32
BF16 = jnp.bfloat16
VMEM = pltpu.MemorySpace.VMEM
SMEM = pltpu.MemorySpace.SMEM


def gelu(x):
    half = 0.5 * x
    inner = x * (0.7978845608028654 + 0.035677408136300125 * (x * x))
    return half + half * jnp.tanh(inner)


def one_hot_columns(columns, shift, source_permuted, target_permuted):
    target = lax.broadcasted_iota(jnp.int32, (columns, columns), 0)
    source = lax.broadcasted_iota(jnp.int32, (columns, columns), 1)
    tiles = columns // SUB
    if target_permuted:
        target = (target % SUB) * tiles + target // SUB
    if source_permuted:
        source = (source % SUB) * tiles + source // SUB
    wanted = (target + shift) & (columns - 1)
    return jnp.where(wanted == source, 1.0, 0.0).astype(BF16)


def store_row(ref, row, value, reach):
    columns = value.shape[0]
    ref[row, PAD * SUB : PAD * SUB + columns, :] = value.astype(BF16)
    for k in range(reach):
        first = value[k * SUB : (k + 1) * SUB]
        at = PAD * SUB + columns + k * SUB
        ref[row, at : at + SUB, :] = pltpu.roll(first, SUB - 1, 0).astype(BF16)
        low = columns - (k + 1) * SUB
        last = value[low : low + SUB]
        at = PAD * SUB - (k + 1) * SUB
        ref[row, at : at + SUB, :] = pltpu.roll(last, 1, 0).astype(BF16)


def place_rows(ref, source, hot, reach):
    count = source.shape[0]
    for k in range(0, count, 2):
        pair = source[k]
        if k + 1 < count:
            pair = jnp.concatenate([pair, source[k + 1]], axis=1)
        moved = jnp.dot(hot, pair, preferred_element_type=F32)
        store_row(ref, k, moved[:, :128], reach)
        if k + 1 < count:
            store_row(ref, k + 1, moved[:, 128:], reach)


def layer_rows(layer, band_rows):
    used = 2 ** (layer + 1) - 1
    return list(range(used, band_rows + 2 * MARGIN - used))


def row_groups(layer, band_rows, size):
    rows = set(layer_rows(layer, band_rows))
    firsts = []
    while rows:
        r = min(rows)
        firsts.append(r)
        rows -= {r, r + 2**layer}
    return [firsts[k : k + size] for k in range(0, len(firsts), size)]


def lead_rows(source, middle, sink, weights, bias, limits, results, band_rows, columns):
    low, high = limits
    steps = [
        (layer, group)
        for layer in range(LAYERS)
        for group in row_groups(layer, band_rows, GROUP)
    ]
    places = [source, middle[0], middle[1]]

    def product(layer, group, out):
        dilation = 2**layer
        stacked = []
        for first in group:
            pieces = []
            for rho in range(4):
                ref, row = places[layer](first + (rho - 1) * dilation)
                for tap in range(3):
                    start = (PAD + (tap - 1) * dilation) * SUB
                    pieces.append(ref[row, start : start + columns, :])
            stacked.append(jnp.concatenate(pieces, axis=1))
        out[: len(group) * columns, :] = jnp.dot(
            jnp.concatenate(stacked, axis=0), weights[layer], preferred_element_type=F32
        )

    def finish(layer, group, got):
        offset = bias[layer][None, :].astype(F32)
        for k, first in enumerate(group):
            for half in range(2):
                at = first + half * 2**layer
                ref, row = places[layer](at)
                kept = ref[row, PAD * SUB : PAD * SUB + columns, :].astype(F32)
                summed = got[k * columns : (k + 1) * columns, half * 128 : half * 128 + 128]
                value = kept + gelu(summed + offset)
                if layer + 1 == LAYERS:
                    sink(at, value)
                    continue
                if at < MARGIN:
                    value = value * low
                elif at >= MARGIN + band_rows:
                    value = value * high
                ref, row = places[layer + 1](at)
                store_row(ref, row, value, 2 ** (layer + 1))

    for k, (layer, group) in enumerate(steps):
        if k and steps[k - 1][0] == layer:
            product(layer, group, results.at[k % 2])
            finish(*steps[k - 1], results.at[(k - 1) % 2])
        else:
            if k:
                finish(*steps[k - 1], results.at[(k - 1) % 2])
            product(layer, group, results.at[k % 2])
    finish(*steps[-1], results.at[(len(steps) - 1) % 2])


def shifts(rotations):
    tile = lax.axis_index("tile")
    tiles = rotations.shape[0]
    own = rotations[tile]
    up = own - rotations[jnp.maximum(tile - 1, 0)]
    down = own - rotations[jnp.minimum(tile + 1, tiles - 1)]
    low = jnp.where(tile > 0, 1.0, 0.0).astype(F32)
    high = jnp.where(tile < tiles - 1, 1.0, 0.0).astype(F32)
    return up, down, (low, high)


def run_lead(
    rotations, own, up, down, weights, bias, up_buf, down_buf, mid_a, mid_b, results, sink, permuted
):
    band_rows, columns = own.shape[0], up.shape[1]
    up_shift, down_shift, limits = shifts(rotations)
    place_rows(up_buf, up, one_hot_columns(columns, up_shift, permuted, True), 1)
    place_rows(down_buf, down, one_hot_columns(columns, down_shift, permuted, True), 1)

    def source(e):
        if e < MARGIN:
            return up_buf, e
        if e < MARGIN + band_rows:
            return own, e - MARGIN
        return down_buf, e - MARGIN - band_rows

    lead_rows(
        source, [lambda e: (mid_a, e), lambda e: (mid_b, e)], sink,
        weights, bias, limits, results, band_rows, columns,
    )


def prep_kernel(own, conv_weight, ocean_weight, field, weights, packed):
    columns = own.shape[1]
    half_rows = ocean_weight.shape[0] // 2
    pack = jnp.concatenate([ocean_weight[:half_rows], ocean_weight[half_rows:]], axis=1)

    def copy(k, carry):
        packed[k] = pack
        return carry

    lax.fori_loop(0, packed.shape[0], copy, 0)
    place_rows(field, own, one_hot_columns(columns, 0, False, True), 1)
    zero = jnp.zeros((384, 128), BF16)
    for layer in range(LAYERS):
        for half in range(2):
            at = (1 - half) * 1152
            weights[layer, at : at + 384, half * 128 : half * 128 + 128] = zero
            for tap in range(9):
                at = half * 384 + tap * 128
                weights[layer, at : at + 128, half * 128 : half * 128 + 128] = conv_weight[
                    layer, tap
                ]


def lead_one_kernel(
    rotations, own, up, down, weights, bias, field, send_up, send_down, *scratch
):
    band_rows = own.shape[0]

    def sink(e, value):
        row = e - MARGIN
        store_row(field, row, value, 1)
        if row < MARGIN:
            send_down[row] = value.astype(BF16)
        if row >= band_rows - MARGIN:
            send_up[row - (band_rows - MARGIN)] = value.astype(BF16)

    run_lead(rotations, own, up, down, weights, bias, *scratch, sink, False)


def table_kernel(gathered, table):
    taps_from = lax.broadcasted_iota(jnp.int32, (96, 512), 0)
    lanes_to = lax.broadcasted_iota(jnp.int32, (96, 512), 1)
    cell = lanes_to // 128
    spread = jnp.where(
        lanes_to % 128 + 32 * (taps_from // 32) - taps_from % 32 == 32 * (cell + 1), 1.0, 0.0
    ).astype(BF16)

    def body(owner, carry):
        pack = gathered[owner]
        taps = jnp.concatenate([pack[:, :64], pack[:, 64:]], axis=0)
        for tap_row in range(3):
            wide = lax.dot_general(
                taps[tap_row * 96 : tap_row * 96 + 96], spread, (((0,), (0,)), ((), ())),
                preferred_element_type=F32,
            )
            for half in range(2):
                for q in range(4):
                    at = tap_row * 256 + half * 128 + q * 32
                    table[owner, at : at + 32, :] = wide[
                        half * 32 : half * 32 + 32, q * 128 : q * 128 + 128
                    ].astype(BF16)
        return carry

    lax.fori_loop(0, gathered.shape[0], body, 0)


def block_lanes(channel_major_rows):
    a = lax.broadcasted_iota(jnp.int32, (512, 512), 0)
    b = lax.broadcasted_iota(jnp.int32, (512, 512), 1)
    src, dst = (a, b) if channel_major_rows else (b, a)
    wanted = (dst % 32) * 16 + dst // 32
    return jnp.where(src == wanted, 1.0, 0.0).astype(BF16)


def lead_two_kernel(
    rotations, own, up, down, weights, bias, force, table, state, owners, sea,
    atmos_out, sea_state, last, joined, acc, *scratch,
):
    band_rows, columns = own.shape[0], up.shape[1]

    def sink(e, value):
        last[e - MARGIN] = value.astype(BF16)

    run_lead(rotations, own, up, down, weights, bias, *scratch, sink, True)
    hot = one_hot_columns(columns, 0, True, False)
    for row in range(0, band_rows, 2):
        moved = jnp.dot(
            hot, jnp.concatenate([last[row], last[row + 1]], axis=1), preferred_element_type=F32
        )
        atmos_out[row] = moved[:, :128].astype(BF16)
        atmos_out[row + 1] = moved[:, 128:].astype(BF16)

    blocks = band_rows // BH * (columns // BW)
    per_half = columns // BW
    wide = force[...]
    zero = jnp.zeros((32, 128), BF16)
    spread = jnp.concatenate(
        [
            jnp.concatenate([wide if q % 4 == p else zero for q in range(8)], axis=1)
            for p in range(4)
        ],
        axis=0,
    )
    forcing = []
    for i in range(BH):
        pieces = []
        for half in range(band_rows // BH):
            row = half * BH + i
            for g in range(SUB // BW):
                cells = []
                for field, pad in ((own, PAD), (last, 0)):
                    for q in range(BW):
                        tile = (pad + g * BW + q) * SUB
                        cells.append(field[row, tile : tile + SUB, :])
                pieces.append(jnp.concatenate(cells, axis=1))
        wide = jnp.concatenate(pieces, axis=0)
        forcing.append(
            (
                0.5
                * lax.dot_general(
                    wide, spread, (((1,), (1,)), ((), ())), preferred_element_type=F32
                )
            ).astype(BF16)
        )
    forcing = jnp.concatenate(forcing, axis=1)
    a = lax.broadcasted_iota(jnp.int32, (blocks, blocks), 0)
    b = lax.broadcasted_iota(jnp.int32, (blocks, blocks), 1)
    source = (a // per_half) * per_half + (a % 4) * SUB + (a % per_half) // 4
    order = jnp.where(source == b, 1.0, 0.0).astype(BF16)
    forcing = jnp.dot(order, forcing, preferred_element_type=F32).astype(BF16)
    own_state = jnp.dot(
        state[...], block_lanes(True), preferred_element_type=F32
    ).astype(BF16)
    joined[...] = jnp.zeros_like(joined)
    for i in range(BH):
        for tap_row in range(3):
            at = i + tap_row - 1
            if 0 <= at < BH:
                here = pl.ds(i * blocks, blocks)
                joined[here, tap_row * 256 : tap_row * 256 + 128] = forcing[
                    :, at * 128 : at * 128 + 128
                ]
                joined[here, tap_row * 256 + 128 : tap_row * 256 + 256] = own_state[
                    :, at * 128 : at * 128 + 128
                ]
    owner = jnp.transpose(jnp.broadcast_to(owners[...], (128, blocks)))

    def body(k, carry):
        pair = jnp.concatenate([table[2 * k], table[2 * k + 1]], axis=1)
        for i in range(BH):
            here = pl.ds(i * blocks, blocks)
            got = jnp.dot(joined[here, :], pair, preferred_element_type=F32)
            old = acc[here, :]
            new = jnp.where(owner == 2 * k, got[:, :128], old)
            acc[here, :] = jnp.where(owner == 2 * k + 1, got[:, 128:], new)
        return carry

    acc[...] = jnp.zeros_like(acc)
    lax.fori_loop(0, table.shape[0] // 2, body, 0)
    fresh = []
    for i in range(BH):
        kept = own_state[:, i * 128 : i * 128 + 128].astype(F32)
        fresh.append((kept + gelu(acc[i * blocks : (i + 1) * blocks, :])).astype(BF16))
    result = jnp.dot(
        jnp.concatenate(fresh, axis=1), block_lanes(False), preferred_element_type=F32
    )
    flag = jnp.transpose(jnp.broadcast_to(sea[...], (128, blocks))) > 0
    for i in range(BH):
        lanes = slice(i * 128, i * 128 + 128)
        sea_state[:, lanes] = jnp.where(flag, result[:, lanes], 0.0).astype(BF16)


def call(kernel, out_shape, scratch, specs, limit):
    return pl.pallas_call(
        kernel,
        out_shape=out_shape,
        in_specs=[pl.BlockSpec(memory_space=s) for s in specs],
        out_specs=jax.tree.map(lambda _: pl.BlockSpec(memory_space=VMEM), out_shape),
        scratch_shapes=scratch,
        compiler_params=pltpu.CompilerParams(vmem_limit_bytes=limit * 2**20),
    )


def here(x):
    return pltpu.with_memory_space_constraint(x, VMEM)


def local(
    atmosphere, ocean_state, land_sea, owners, rotations,
    conv_weight, conv_bias, force_weight, ocean_weight,
):
    tiles = lax.axis_size("tile")
    band_rows, columns, channels = atmosphere.shape
    blocks = owners.shape[0]
    shape = jax.ShapeDtypeStruct
    up_pairs = [(i, i + 1) for i in range(tiles - 1)]
    down_pairs = [(j, i) for i, j in up_pairs]

    up = lax.ppermute(atmosphere[band_rows - MARGIN :], "tile", up_pairs)
    down = lax.ppermute(atmosphere[:MARGIN], "tile", down_pairs)

    padded = columns + 2 * PAD * SUB
    own, weights, packed = call(
        prep_kernel,
        (
            pltpu.VMEM((band_rows, padded, channels), BF16),
            pltpu.VMEM((LAYERS, 1536, 256), BF16),
            pltpu.VMEM((tiles, 144, 128), BF16),
        ),
        [], [VMEM] * 3, 12,
    )(atmosphere, conv_weight, jnp.swapaxes(ocean_weight[0], 1, 2).reshape(-1, 64))
    own, weights = here(own), here(weights)
    gathered = lax.all_to_all(packed, "tile", 0, 0, tiled=True)

    scratch = [
        pltpu.VMEM((MARGIN, padded, channels), BF16),
        pltpu.VMEM((MARGIN, padded, channels), BF16),
        pltpu.VMEM((band_rows + 2 * MARGIN, padded, channels), BF16),
        pltpu.VMEM((band_rows + 2 * MARGIN, padded, channels), BF16),
        pltpu.VMEM((2, GROUP * columns, 256), F32),
    ]
    halo = pltpu.VMEM((MARGIN, columns, channels), BF16)
    lead_one, send_up, send_down = call(
        lead_one_kernel,
        (pltpu.VMEM((band_rows, padded, channels), BF16), halo, halo),
        scratch, [SMEM] + [VMEM] * 5, 16,
    )(rotations, own, here(up), here(down), weights, conv_bias)

    up = lax.ppermute(send_up, "tile", up_pairs)
    down = lax.ppermute(send_down, "tile", down_pairs)

    table = call(table_kernel, pltpu.VMEM((tiles, 768, 128), BF16), [], [VMEM], 8)(here(gathered))

    return call(
        lead_two_kernel,
        (shape(atmosphere.shape, BF16), shape(ocean_state.shape, BF16)),
        [
            pltpu.VMEM((band_rows, columns, channels), BF16),
            pltpu.VMEM((BH * blocks, 768), BF16),
            pltpu.VMEM((BH * blocks, 128), F32),
        ]
        + scratch,
        [SMEM] + [VMEM] * 10, 20,
    )(
        rotations, here(lead_one), here(up), here(down), weights, conv_bias, force_weight.T, here(table),
        ocean_state, owners.reshape(1, blocks), land_sea.reshape(1, blocks),
    )


def solution(mesh):
    in_specs = (
        P(("ens", "tile"), None, None),
        P(("ens", "tile"), None),
        P("tile"),
        P("tile", None),
        P(),
        P(),
        P(),
        P(),
        P("tile", None, None, None),
    )
    out_specs = (P(("ens", "tile"), None, None), P(("ens", "tile"), None))

    return jax.shard_map(local, mesh=mesh, in_specs=in_specs, out_specs=out_specs, check_vma=False)
```

time: 83.4 us -> 72.8 us (0.87)
  the two profiles are of different devices: /device:TPU:16 before, /device:TPU:19 now
where the time goes in v1:
time: 72.8 us; the launch traced here: 72.3 us
  Pallas kernels  25.5 us (35%)
  waiting for transfers between devices  19.2 us (26%)
  starting transfers between devices  18.5 us (25%)
  local copies, waits for them, and re-layouts  8.33 us (11%)
  between operations  0.76 us (1%)
    pallas_call x1, Pallas kernels, local(): call(lead_two_kernel, (shape(atmosphere.shape, BF16), shape(ocean_state.s...  12.7 us
    unnamed x30, local copies, waits for them, and re-layouts  8.17 us
    pallas_call x1, Pallas kernels, local(): call(lead_one_kernel, (pltpu.VMEM((band_rows, padded, channels), BF16), h...  7.72 us
    ppermute x1, waiting for transfers between devices, local(): down = lax.ppermute(atmosphere[:MARGIN], 'tile', down_pairs)  7.38 us
    all_to_all x1, starting transfers between devices, local(): gathered = lax.all_to_all(packed, 'tile', 0, 0, tiled=True)  6.47 us
    ppermute x1, waiting for transfers between devices, local(): up = lax.ppermute(atmosphere[band_rows - MARGIN:], 'tile', up_pairs)  5.7 us
    ppermute x1, starting transfers between devices, local(): up = lax.ppermute(send_up, 'tile', up_pairs)  4.38 us
    pallas_call x1, Pallas kernels, local(): call(table_kernel, pltpu.VMEM((tiles, 768, 128), BF16), [], [VMEM], 8)  4.36 us
  transfers between devices with their start and end apart: 5, of which 4 were waited for; matrix products, arithmetic and copies ran while one was open for 0% of the time, Pallas kernels for 17%

profile of v1, /device:TPU:19, one launch (start us, length us, event | category | flops | bytes accessed | tf_op | source)
XLA Modules:
  0.0 72.3 jit_solution(2835269530356064389)
XLA Ops:
  0.6 0.0 copy-start.11
  0.6 0.0 copy-start.12
  0.7 0.0 copy-start
  0.7 1.0 %copy-done = bf16[8,256,128]{2,1,0:T(8,128)(2,1)S(1)} copy-done((bf16[8,256,128]{2,1,0:T(8,128)(2,1)S(1)}, bf16[8,256,128]{2,1,0:T(8,128)(2,1)}, u32[]{:S(2)}) %copy-start) | copy-done | bytes 524312
  1.7 1.2 %copy-done.2 = bf16[3,9,128,128]{3,2,1,0:T(8,128)(2,1)S(1)} copy-done((bf16[3,9,128,128]{3,2,1,0:T(8,128)(2,1)S(1)}, bf16[3,9,128,128]{3,2,1,0:T(8,128)(2,1)}, u32[]{:S(2)}) %copy-start.2) | copy-done | bytes 884760
  2.9 0.9 %copy-done.9 = bf16[1,9,64,32]{2,3,1,0:T(8,128)(2,1)S(1)} copy-done((bf16[1,9,64,32]{2,3,1,0:T(8,128)(2,1)S(1)}, bf16[1,9,64,32]{2,3,1,0:T(8,128)(2,1)}, u32[]{:S(2)}) %copy-start.9) | copy-done | bytes 36888
  3.8 0.7 %shard_map.104 = (bf16[8,384,128]{2,1,0:T(8,128)(2,1)S(1)}, bf16[3,1536,256]{2,1,0:T(8,128)(2,1)S(1)}, bf16[16,144,128]{2,1,0:T(8,128)(2,1)S(1)}) custom-call(bf16[8,256,128]{2,1,0:T(8,128)(2,1)S(1)} %copy-done, bf16[3,9,128,128]{3,2,1,0:T(8,128)(2,1)S(1)} %copy-done.2, bf16[288,64]{1,0:T(8,128)(2,1)S(1)} %bitcast.8), custom_call_target="tpu_custom_call" | custom-call | tf_op jit(solution)/shard_map/pallas_call | solution.py:368
  4.5 0.0 copy-start.3
  4.5 0.9 %copy-done.3 = bf16[8,384,128]{2,1,0:T(8,128)(2,1)} copy-done((bf16[8,384,128]{2,1,0:T(8,128)(2,1)}, bf16[8,384,128]{2,1,0:T(8,128)(2,1)S(1)}, u32[]{:S(2)}) %copy-start.3) | copy-done | bytes 786456
  5.4 0.8 %copy-done.7 = bf16[16,144,128]{2,1,0:T(8,128)(2,1)} copy-done((bf16[16,144,128]{2,1,0:T(8,128)(2,1)}, bf16[16,144,128]{2,1,0:T(8,128)(2,1)S(1)}, u32[]{:S(2)}) %copy-start.7) | copy-done | bytes 589848
  6.2 6.5 %all-to-all-start = ((bf16[16,144,128]{2,1,0:T(8,128)(2,1)}), bf16[16,144,128]{2,1,0:T(8,128)(2,1)S(1)}, u32[]{:S(2)}, u32[]{:S(2)}) async-start(bf16[16,144,128]{2,1,0:T(8,128)(2,1)} %copy-done.7), calls=%async_computation | async-start | bytes 1179648 | tf_op jit(solution)/shard_map/all_to_all | solution.py:378
  12.7 0.0 copy-done.1
  12.7 0.2 fusion
  12.9 2.3 %collective-permute-start.1 = (bf16[7,256,128]{2,1,0:T(8,128)(2,1)S(1)}, bf16[7,256,128]{2,1,0:T(8,128)(2,1)S(1)}, u32[]{:S(2)}, u32[]{:S(2)}) collective-permute-start(bf16[7,256,128]{2,1,0:T(8,128)(2,1)S(1)} %get-tuple-element.14), channel_id=1, source_target_pairs={{1,0},{2,1},{3,2},{4,3},{5,4},{6,5},{7,6},{8,7},{9,8},{10,9},{11,1... | collective-permute-start | bytes 1376264 | tf_op jit(solution)/shard_map/ppermute | solution.py:365
  15.2 3.3 %collective-permute-start = (bf16[7,256,128]{2,1,0:T(8,128)(2,1)S(1)}, bf16[7,256,128]{2,1,0:T(8,128)(2,1)S(1)}, u32[]{:S(2)}, u32[]{:S(2)}) collective-permute-start(bf16[7,256,128]{2,1,0:T(8,128)(2,1)S(1)} %get-tuple-element.15), channel_id=1, source_target_pairs={{0,1},{1,2},{2,3},{3,4},{4,5},{5,6},{6,7},{7,8},{8,9},{9,10},{10,1... | collective-permute-start | bytes 1376264 | tf_op jit(solution)/shard_map/ppermute | solution.py:364
  18.5 7.4 %collective-permute-done.1.down = bf16[7,256,128]{2,1,0:T(8,128)(2,1)S(1)} collective-permute-done((bf16[7,256,128]{2,1,0:T(8,128)(2,1)S(1)}, bf16[7,256,128]{2,1,0:T(8,128)(2,1)S(1)}, u32[]{:S(2)}, u32[]{:S(2)}) %collective-permute-start.1) | collective-permute-done | bytes 458784 | tf_op jit(solution)/shard_map/ppermute | solution.py:365
  25.8 5.7 %collective-permute-done.up = bf16[7,256,128]{2,1,0:T(8,128)(2,1)S(1)} collective-permute-done((bf16[7,256,128]{2,1,0:T(8,128)(2,1)S(1)}, bf16[7,256,128]{2,1,0:T(8,128)(2,1)S(1)}, u32[]{:S(2)}, u32[]{:S(2)}) %collective-permute-start) | collective-permute-done | bytes 458784 | tf_op jit(solution)/shard_map/ppermute | solution.py:364
  31.5 0.0 copy-done.11
  31.5 1.1 %copy-done.4 = bf16[8,384,128]{2,1,0:T(8,128)(2,1)S(1)} copy-done((bf16[8,384,128]{2,1,0:T(8,128)(2,1)S(1)}, bf16[8,384,128]{2,1,0:T(8,128)(2,1)}, u32[]{:S(2)}) %copy-start.4) | copy-done | bytes 786456
  32.7 7.7 %shard_map.105 = (bf16[8,384,128]{2,1,0:T(8,128)(2,1)S(1)}, bf16[7,256,128]{2,1,0:T(8,128)(2,1)}, bf16[7,256,128]{2,1,0:T(8,128)(2,1)}) custom-call(s32[16]{0:T(128)S(1)} %copy-done.12, bf16[8,384,128]{2,1,0:T(8,128)(2,1)S(1)} %copy-done.4, bf16[7,256,128]{2,1,0:T(8,128)(2,1)S(1)} %collective-permute-done.up, ...), custom_call_target="tpu_custom_call" | custom-call | tf_op jit(solution)/shard_map/pallas_call | solution.py:388
  40.4 0.9 %copy-done.5 = bf16[8,384,128]{2,1,0:T(8,128)(2,1)} copy-done((bf16[8,384,128]{2,1,0:T(8,128)(2,1)}, bf16[8,384,128]{2,1,0:T(8,128)(2,1)S(1)}, u32[]{:S(2)}) %copy-start.5) | copy-done | bytes 786456
  41.3 4.4 %collective-permute-start.2 = (bf16[7,256,128]{2,1,0:T(8,128)(2,1)}, bf16[7,256,128]{2,1,0:T(8,128)(2,1)S(1)}, u32[]{:S(2)}, u32[]{:S(2)}) collective-permute-start(bf16[7,256,128]{2,1,0:T(8,128)(2,1)} %get-tuple-element.11), channel_id=1, source_target_pairs={{0,1},{1,2},{2,3},{3,4},{4,5},{5,6},{6,7},{7,8},{8,9},{9,10},{10,1... | collective-permute-start | bytes 1376264 | tf_op jit(solution)/shard_map/ppermute | solution.py:394
  45.7 2.1 %collective-permute-start.3 = (bf16[7,256,128]{2,1,0:T(8,128)(2,1)}, bf16[7,256,128]{2,1,0:T(8,128)(2,1)}, u32[]{:S(2)}, u32[]{:S(2)}) collective-permute-start(bf16[7,256,128]{2,1,0:T(8,128)(2,1)} %get-tuple-element.12), channel_id=1, source_target_pairs={{1,0},{2,1},{3,2},{4,3},{5,4},{6,5},{7,6},{8,7},{9,8},{10,9},{11,1... | collective-permute-start | bytes 1376264 | tf_op jit(solution)/shard_map/ppermute | solution.py:395
  47.8 0.0 all-to-all-done.gathered
  47.8 4.4 %shard_map.106.table = bf16[16,768,128]{2,1,0:T(8,128)(2,1)S(1)} custom-call(bf16[16,144,128]{2,1,0:T(8,128)(2,1)S(1)} %all-to-all-done.gathered), custom_call_target="tpu_custom_call" | custom-call | tf_op jit(solution)/shard_map/pallas_call | solution.py:397
  52.2 4.1 %collective-permute-done.2.up = bf16[7,256,128]{2,1,0:T(8,128)(2,1)S(1)} collective-permute-done((bf16[7,256,128]{2,1,0:T(8,128)(2,1)}, bf16[7,256,128]{2,1,0:T(8,128)(2,1)S(1)}, u32[]{:S(2)}, u32[]{:S(2)}) %collective-permute-start.2) | collective-permute-done | bytes 458784 | tf_op jit(solution)/shard_map/ppermute | solution.py:394
  56.3 2.0 %collective-permute-done.3.down = bf16[7,256,128]{2,1,0:T(8,128)(2,1)} collective-permute-done((bf16[7,256,128]{2,1,0:T(8,128)(2,1)}, bf16[7,256,128]{2,1,0:T(8,128)(2,1)}, u32[]{:S(2)}, u32[]{:S(2)}) %collective-permute-start.3) | collective-permute-done | bytes 458784 | tf_op jit(solution)/shard_map/ppermute | solution.py:395
  58.3 0.0 copy-done.6
  58.3 0.0 copy-start.13
  58.3 0.6 copy-done.13
  58.9 0.7 copy-done.14
  59.6 12.7 %shard_map.107 = (bf16[8,256,128]{2,1,0:T(8,128)(2,1)}, bf16[128,512]{1,0:T(8,128)(2,1)}) custom-call(s32[16]{0:T(128)S(1)} %copy-done.12, bf16[8,384,128]{2,1,0:T(8,128)(2,1)S(1)} %copy-done.6, bf16[7,256,128]{2,1,0:T(8,128)(2,1)S(1)} %collective-permute-done.2.up, bf16[7,256,128]{2,1,0:T(8,128)(2,1)} %collective-permute-done.3.down, ...), custom_call_target="tpu_custom_call" | custom-call | tf_op jit(solution)/shard_map/pallas_call | solution.py:399
  (13 shorter events, 0.0 us)
Async XLA Ops:
  0.6 30.9 %copy-start.11 = (bf16[3,128]{1,0:T(4,128)(2,1)S(1)}, bf16[3,128]{1,0:T(4,128)(2,1)}, u32[]{:S(2)}) copy-start(bf16[3,128]{1,0:T(4,128)(2,1)} %bias.3) | copy-start | bytes 2308
  0.6 30.9 %copy-start.12 = (s32[16]{0:T(128)S(1)}, s32[16]{0:T(128)}, u32[]{:S(2)}) copy-start(s32[16]{0:T(128)} %rotations.3) | copy-start | bytes 196
  0.7 1.1 %copy-start = (bf16[8,256,128]{2,1,0:T(8,128)(2,1)S(1)}, bf16[8,256,128]{2,1,0:T(8,128)(2,1)}, u32[]{:S(2)}) copy-start(bf16[8,256,128]{2,1,0:T(8,128)(2,1)} %own.1) | copy-start | bytes 1572868
  1.7 1.2 %copy-start.2 = (bf16[3,9,128,128]{3,2,1,0:T(8,128)(2,1)S(1)}, bf16[3,9,128,128]{3,2,1,0:T(8,128)(2,1)}, u32[]{:S(2)}) copy-start(bf16[3,9,128,128]{3,2,1,0:T(8,128)(2,1)} %conv_weight.1) | copy-start | bytes 2654212
  2.9 0.9 %copy-start.9 = (bf16[1,9,64,32]{2,3,1,0:T(8,128)(2,1)S(1)}, bf16[1,9,64,32]{2,3,1,0:T(8,128)(2,1)}, u32[]{:S(2)}) copy-start(bf16[1,9,64,32]{2,3,1,0:T(8,128)(2,1)} %param.17) | copy-start | bytes 110596
  3.8 8.9 %copy-start.1 = (bf16[8,256,128]{2,1,0:T(8,128)(2,1)S(1)}, bf16[8,256,128]{2,1,0:T(8,128)(2,1)}, u32[]{:S(2)}) copy-start(bf16[8,256,128]{2,1,0:T(8,128)(2,1)} %own.1) | copy-start | bytes 1572868
  4.5 0.9 %copy-start.3 = (bf16[8,384,128]{2,1,0:T(8,128)(2,1)}, bf16[8,384,128]{2,1,0:T(8,128)(2,1)S(1)}, u32[]{:S(2)}) copy-start(bf16[8,384,128]{2,1,0:T(8,128)(2,1)S(1)} %get-tuple-element.8.own) | copy-start | bytes 2359300
  5.4 0.8 %copy-start.7 = (bf16[16,144,128]{2,1,0:T(8,128)(2,1)}, bf16[16,144,128]{2,1,0:T(8,128)(2,1)S(1)}, u32[]{:S(2)}) copy-start(bf16[16,144,128]{2,1,0:T(8,128)(2,1)S(1)} %get-tuple-element.13) | copy-start | bytes 1769476
  6.2 41.6 %all-to-all-start = ((bf16[16,144,128]{2,1,0:T(8,128)(2,1)}), bf16[16,144,128]{2,1,0:T(8,128)(2,1)S(1)}, u32[]{:S(2)}, u32[]{:S(2)}) async-start(bf16[16,144,128]{2,1,0:T(8,128)(2,1)} %copy-done.7), calls=%async_computation | async-start | bytes 1179648 | tf_op jit(solution)/shard_map/all_to_all | solution.py:378
  12.9 13.0 %collective-permute-start.1 = (bf16[7,256,128]{2,1,0:T(8,128)(2,1)S(1)}, bf16[7,256,128]{2,1,0:T(8,128)(2,1)S(1)}, u32[]{:S(2)}, u32[]{:S(2)}) collective-permute-start(bf16[7,256,128]{2,1,0:T(8,128)(2,1)S(1)} %get-tuple-element.14), channel_id=1, source_target_pairs={{1,0},{2,1},{3,2},{4,3},{5,4},{6,5},{7,6},{8,7},{9,8},{10,9},{11,1... | collective-permute-start | bytes 1376264 | tf_op jit(solution)/shard_map/ppermute | solution.py:365
  15.2 16.3 %collective-permute-start = (bf16[7,256,128]{2,1,0:T(8,128)(2,1)S(1)}, bf16[7,256,128]{2,1,0:T(8,128)(2,1)S(1)}, u32[]{:S(2)}, u32[]{:S(2)}) collective-permute-start(bf16[7,256,128]{2,1,0:T(8,128)(2,1)S(1)} %get-tuple-element.15), channel_id=1, source_target_pairs={{0,1},{1,2},{2,3},{3,4},{4,5},{5,6},{6,7},{7,8},{8,9},{9,10},{10,1... | collective-permute-start | bytes 1376264 | tf_op jit(solution)/shard_map/ppermute | solution.py:364
  31.5 1.1 %copy-start.4 = (bf16[8,384,128]{2,1,0:T(8,128)(2,1)S(1)}, bf16[8,384,128]{2,1,0:T(8,128)(2,1)}, u32[]{:S(2)}) copy-start(bf16[8,384,128]{2,1,0:T(8,128)(2,1)} %copy-done.3) | copy-start | bytes 2359300
  32.7 25.6 %copy-start.8 = (bf16[128,512]{1,0:T(8,128)(2,1)S(1)}, bf16[128,512]{1,0:T(8,128)(2,1)}, u32[]{:S(2)}) copy-start(bf16[128,512]{1,0:T(8,128)(2,1)} %state.1) | copy-start | bytes 393220
  32.7 25.6 %copy-start.10 = (bf16[128,32]{0,1:T(8,128)(2,1)S(1)}, bf16[128,32]{0,1:T(8,128)(2,1)}, u32[]{:S(2)}) copy-start(bf16[128,32]{0,1:T(8,128)(2,1)} %param.16) | copy-start | bytes 24580
  40.4 0.9 %copy-start.5 = (bf16[8,384,128]{2,1,0:T(8,128)(2,1)}, bf16[8,384,128]{2,1,0:T(8,128)(2,1)S(1)}, u32[]{:S(2)}) copy-start(bf16[8,384,128]{2,1,0:T(8,128)(2,1)S(1)} %get-tuple-element.10.own) | copy-start | bytes 2359300
  41.3 15.0 %collective-permute-start.2 = (bf16[7,256,128]{2,1,0:T(8,128)(2,1)}, bf16[7,256,128]{2,1,0:T(8,128)(2,1)S(1)}, u32[]{:S(2)}, u32[]{:S(2)}) collective-permute-start(bf16[7,256,128]{2,1,0:T(8,128)(2,1)} %get-tuple-element.11), channel_id=1, source_target_pairs={{0,1},{1,2},{2,3},{3,4},{4,5},{5,6},{6,7},{7,8},{8,9},{9,10},{10,1... | collective-permute-start | bytes 1376264 | tf_op jit(solution)/shard_map/ppermute | solution.py:394
  45.7 12.6 %collective-permute-start.3 = (bf16[7,256,128]{2,1,0:T(8,128)(2,1)}, bf16[7,256,128]{2,1,0:T(8,128)(2,1)}, u32[]{:S(2)}, u32[]{:S(2)}) collective-permute-start(bf16[7,256,128]{2,1,0:T(8,128)(2,1)} %get-tuple-element.12), channel_id=1, source_target_pairs={{1,0},{2,1},{3,2},{4,3},{5,4},{6,5},{7,6},{8,7},{9,8},{10,9},{11,1... | collective-permute-start | bytes 1376264 | tf_op jit(solution)/shard_map/ppermute | solution.py:395
  47.8 10.5 %copy-start.6 = (bf16[8,384,128]{2,1,0:T(8,128)(2,1)S(1)}, bf16[8,384,128]{2,1,0:T(8,128)(2,1)}, u32[]{:S(2)}) copy-start(bf16[8,384,128]{2,1,0:T(8,128)(2,1)} %copy-done.5) | copy-start | bytes 2359300
  58.3 0.7 copy-start.13
  58.9 0.7 copy-start.14

commit v2 on v1

v2 whole, which is shorter than its diff:
```python
import jax
import jax.numpy as jnp
from jax import lax
from jax.experimental import pallas as pl
from jax.experimental.pallas import tpu as pltpu
from jax.sharding import PartitionSpec as P


LAYERS = 3
BH = 4
BW = 4
SUB = 16
PAD = 4
GROUP = 2
MARGIN = 2**LAYERS - 1
F32 = jnp.float32
BF16 = jnp.bfloat16
VMEM = pltpu.MemorySpace.VMEM
SMEM = pltpu.MemorySpace.SMEM


def gelu(x):
    half = 0.5 * x
    inner = x * (0.7978845608028654 + 0.035677408136300125 * (x * x))
    return half + half * jnp.tanh(inner)


def one_hot_columns(columns, shift, source_permuted, target_permuted):
    target = lax.broadcasted_iota(jnp.int32, (columns, columns), 0)
    source = lax.broadcasted_iota(jnp.int32, (columns, columns), 1)
    tiles = columns // SUB
    if target_permuted:
        target = (target % SUB) * tiles + target // SUB
    if source_permuted:
        source = (source % SUB) * tiles + source // SUB
    wanted = (target + shift) & (columns - 1)
    return jnp.where(wanted == source, 1.0, 0.0).astype(BF16)


def store_row(ref, row, value, reach):
    columns = value.shape[0]
    ref[row, PAD * SUB : PAD * SUB + columns, :] = value.astype(BF16)
    for k in range(reach):
        first = value[k * SUB : (k + 1) * SUB]
        at = PAD * SUB + columns + k * SUB
        ref[row, at : at + SUB, :] = pltpu.roll(first, SUB - 1, 0).astype(BF16)
        low = columns - (k + 1) * SUB
        last = value[low : low + SUB]
        at = PAD * SUB - (k + 1) * SUB
        ref[row, at : at + SUB, :] = pltpu.roll(last, 1, 0).astype(BF16)


def layer_rows(layer, band_rows):
    used = 2 ** (layer + 1) - 1
    return list(range(used, band_rows + 2 * MARGIN - used))


def row_groups(rows, dilation, size):
    rows = set(rows)
    firsts = []
    while rows:
        r = min(rows)
        firsts.append(r)
        rows -= {r, r + dilation}
    return [firsts[k : k + size] for k in range(0, len(firsts), size)]


def rotate_kernel(rotations, own, field, send_up, send_down):
    band_rows, columns = own.shape[0], own.shape[1]
    hot = one_hot_columns(columns, -rotations[lax.axis_index("tile")], False, True)
    for k in range(0, band_rows, 2):
        moved = jnp.dot(
            hot, jnp.concatenate([own[k], own[k + 1]], axis=1), preferred_element_type=F32
        )
        for half in range(2):
            give_row(k + half, moved[:, half * 128 : half * 128 + 128], field, send_up, send_down)


def give_row(row, value, field, send_up, send_down):
    band_rows = field.shape[0]
    store_row(field, row, value, 1)
    if row < MARGIN:
        send_down[row] = value.astype(BF16)
    if row >= band_rows - MARGIN:
        send_up[row - (band_rows - MARGIN)] = value.astype(BF16)


def pack_kernel(ocean_weight, packed):
    half_rows = ocean_weight.shape[0] // 2
    pack = jnp.concatenate([ocean_weight[:half_rows], ocean_weight[half_rows:]], axis=1)

    def copy(k, carry):
        packed[k] = pack
        return carry

    lax.fori_loop(0, packed.shape[0], copy, 0)


def pair_weights(conv_weight, weights):
    zero = jnp.zeros((384, 128), BF16)
    for layer in range(LAYERS):
        for half in range(2):
            at = (1 - half) * 1152
            weights[layer, at : at + 384, half * 128 : half * 128 + 128] = zero
            for tap in range(9):
                at = half * 384 + tap * 128
                weights[layer, at : at + 128, half * 128 : half * 128 + 128] = conv_weight[
                    layer, tap
                ]


def conv_rows(plan, place, sink, weights, bias, results, band_rows, columns):
    tile = lax.axis_index("tile")
    low = jnp.where(tile > 0, 1.0, 0.0).astype(F32)
    high = jnp.where(tile < lax.axis_size("tile") - 1, 1.0, 0.0).astype(F32)

    def piece(ref, row, moved):
        padded = ref.shape[1] > columns
        if padded or moved == 0:
            start = (PAD * SUB if padded else 0) + moved * SUB
            return ref[row, start : start + columns, :]
        edge = ref[row, columns - SUB :, :] if moved < 0 else ref[row, :SUB, :]
        edge = pltpu.roll(edge.astype(F32), 1 if moved < 0 else SUB - 1, 0).astype(BF16)
        if moved < 0:
            return jnp.concatenate([edge, ref[row, : columns - SUB, :]], axis=0)
        return jnp.concatenate([ref[row, SUB:, :], edge], axis=0)

    def product(layer, group, out):
        dilation = 2**layer
        stacked = []
        for first in group:
            pieces = []
            for rho in range(4):
                ref, row = place(layer, first + (rho - 1) * dilation)
                for tap in range(3):
                    pieces.append(piece(ref, row, (tap - 1) * dilation))
            stacked.append(jnp.concatenate(pieces, axis=1))
        out[: len(group) * columns, :] = jnp.dot(
            jnp.concatenate(stacked, axis=0), weights[layer], preferred_element_type=F32
        )

    def finish(layer, group, got):
        offset = bias[layer][None, :].astype(F32)
        for k, first in enumerate(group):
            for half in range(2):
                at = first + half * 2**layer
                ref, row = place(layer, at)
                kept = piece(ref, row, 0).astype(F32)
                summed = got[k * columns : (k + 1) * columns, half * 128 : half * 128 + 128]
                value = kept + gelu(summed + offset)
                if layer + 1 == LAYERS:
                    sink(at, value)
                    continue
                if at < MARGIN:
                    value = value * low
                elif at >= MARGIN + band_rows:
                    value = value * high
                ref, row = place(layer + 1, at)
                store_row(ref, row, value, 2 ** (layer + 1))

    for k, (layer, group) in enumerate(plan):
        if k and plan[k - 1][0] == layer:
            product(layer, group, results.at[k % 2])
            finish(*plan[k - 1], results.at[(k - 1) % 2])
        else:
            if k:
                finish(*plan[k - 1], results.at[(k - 1) % 2])
            product(layer, group, results.at[k % 2])
    finish(*plan[-1], results.at[(len(plan) - 1) % 2])


def plans(band_rows):
    edge = MARGIN + band_rows
    ready = edge - 1
    whole, early, late = [], [], []
    for layer in range(LAYERS):
        dilation = 2**layer
        rows = layer_rows(layer, band_rows)
        whole += [(layer, g) for g in row_groups(rows, dilation, GROUP)]
        ready -= dilation
        first = [r for r in rows if r <= ready]
        first = first[: len(first) // (2 * dilation) * 2 * dilation]
        ready = first[-1] if first else 0
        early += [(layer, g) for g in row_groups(first, dilation, GROUP)]
        rest = [r for r in rows if r not in first]
        late += [(layer, g) for g in row_groups(rest, dilation, GROUP)]
    return whole, early, late


def pick(own, up, down, e):
    band_rows = own.shape[0]
    if e < MARGIN:
        return up, e
    if e < MARGIN + band_rows:
        return own, e - MARGIN
    return down, e - MARGIN - band_rows


def lead_one_kernel(
    own, up, down, weights, bias, field, send_up, send_down, mid_a, mid_b, results
):
    band_rows, columns = own.shape[0], up.shape[1]

    def place(layer, e):
        if layer == 0:
            return pick(own, up, down, e)
        return (mid_a, mid_b)[layer - 1], e

    def sink(e, value):
        give_row(e - MARGIN, value, field, send_up, send_down)

    conv_rows(
        plans(band_rows)[0], place, sink, weights, bias, results, band_rows, columns
    )


def early_kernel(own, up, weights, bias, top_a, top_b, results):
    band_rows, columns = own.shape[0], up.shape[1]

    def place(layer, e):
        if layer == 0:
            return pick(own, up, None, e)
        return (top_a, top_b)[layer - 1], e

    conv_rows(
        plans(band_rows)[1], place, None, weights, bias, results, band_rows, columns
    )


def table_kernel(
    gathered, conv_weight, state, owners, sea,
    weights, table, spread_state, kept_state, unspread, owner_of, sea_of,
):
    pair_weights(conv_weight, weights)
    blocks = state.shape[0]
    owner_of[...] = jnp.transpose(jnp.broadcast_to(owners[...], (128, blocks)))
    sea_of[...] = jnp.transpose(jnp.broadcast_to(sea[...], (128, blocks)))

    a = lax.broadcasted_iota(jnp.int32, (512, 512), 0)
    b = lax.broadcasted_iota(jnp.int32, (512, 512), 1)
    unspread[...] = jnp.where(a == ((b & 15) << 5) + (b >> 4), 1.0, 0.0).astype(BF16)
    spread = jnp.where(((b & 31) << 4) + (b >> 5) == a, 1.0, 0.0).astype(BF16)
    kept = jnp.dot(state[...], spread, preferred_element_type=F32).astype(BF16)
    kept_state[...] = kept
    zero = jnp.zeros((blocks, 32), BF16)
    for i in range(BH):
        cells = []
        for q in range(BW):
            at = (i * BW + q) * 32
            cells += [zero, kept[:, at : at + 32]]
        spread_state[:, i * 256 : i * 256 + 256] = jnp.concatenate(cells, axis=1)

    left = lax.broadcasted_iota(jnp.int32, (32, 128), 1) < 64
    nothing = jnp.zeros((32, 128), BF16)

    def body(owner, carry):
        pack = gathered[owner]
        other = pltpu.roll(pack.astype(F32), 64, 1).astype(BF16)

        def tap_at(t, right):
            if t < 4:
                return (other if right else pack)[t * 32 : t * 32 + 32]
            if t > 4:
                return (pack if right else other)[t * 32 - 144 : t * 32 - 112]
            first, second = (other, pack) if right else (pack, other)
            return jnp.concatenate([first[128:144], second[:16]], axis=0)

        for tap_row in range(3):
            for j in range(BW):
                for pair in range(BW // 2):
                    b = 2 * pair - j + 1
                    one = tap_at(tap_row * 3 + b, False) if 0 <= b < 3 else nothing
                    two = tap_at(tap_row * 3 + b + 1, True) if 0 <= b + 1 < 3 else nothing
                    at = tap_row * 256 + pair * 128
                    table[owner, j * 32 : j * 32 + 32, at : at + 128] = jnp.where(left, one, two)
        return carry

    lax.fori_loop(0, gathered.shape[0], body, 0)


def late_kernel(
    rotations, own, up, down, top_a, top_b, weights, bias, force, table,
    spread_state, kept_state, unspread, owner_of, sea_of,
    atmos_out, sea_state, mid_a, mid_b, results, last, joined, acc,
):
    band_rows, columns = own.shape[0], up.shape[1]
    _, early, late = plans(band_rows)
    firsts = [
        {r for l, g in early for f in g for r in (f, f + 2**l) if l == layer}
        for layer in range(LAYERS)
    ]

    def place(layer, e):
        if layer == 0:
            return pick(own, up, down, e)
        if e in firsts[layer - 1]:
            return (top_a, top_b)[layer - 1], e
        return (mid_a, mid_b)[layer - 1], e

    def sink(e, value):
        last[e - MARGIN] = value.astype(BF16)

    conv_rows(late, place, sink, weights, bias, results, band_rows, columns)

    shift = rotations[lax.axis_index("tile")]
    hot = one_hot_columns(columns, shift, True, False)
    for row in range(0, band_rows, 2):
        moved = jnp.dot(
            hot, jnp.concatenate([last[row], last[row + 1]], axis=1), preferred_element_type=F32
        )
        atmos_out[row] = moved[:, :128].astype(BF16)
        atmos_out[row + 1] = moved[:, 128:].astype(BF16)

    wide = force[...]
    none = jnp.zeros_like(wide)
    repeated = jnp.concatenate([wide, none] * BW, axis=0)
    repeated = jnp.concatenate([repeated, repeated], axis=1)
    per_half = columns // BW
    cells = lax.broadcasted_iota(jnp.int32, (columns, columns), 0)
    stored = lax.broadcasted_iota(jnp.int32, (columns, columns), 1)
    wanted = ((cells % per_half) * BW + cells // per_half + shift) & (columns - 1)
    gather = jnp.where(
        wanted == (stored % SUB) * (columns // SUB) + stored // SUB, 1.0, 0.0
    ).astype(BF16)
    lane = lax.broadcasted_iota(jnp.int32, (per_half, 256), 1) // 64
    blocks = band_rows // BH * per_half
    joined[...] = jnp.zeros_like(joined)
    for row in range(band_rows):
        both = jnp.concatenate(
            [own[row, PAD * SUB : PAD * SUB + columns, :], last[row]], axis=1
        )
        forcing = (
            0.5
            * lax.dot_general(both, repeated, (((1,), (1,)), ((), ())), preferred_element_type=F32)
        ).astype(BF16)
        spots = jnp.dot(gather, forcing, preferred_element_type=F32)
        mine = spots[:per_half]
        for q in range(1, BW):
            mine = jnp.where(lane == q, spots[q * per_half : (q + 1) * per_half], mine)
        half, i = row // BH, row % BH
        first = half * per_half
        mine = (
            mine + spread_state[first : first + per_half, i * 256 : i * 256 + 256].astype(F32)
        ).astype(BF16)
        for tap_row in range(3):
            to = i - tap_row + 1
            if 0 <= to < BH:
                joined[
                    to * blocks + first : to * blocks + first + per_half,
                    tap_row * 256 : tap_row * 256 + 256,
                ] = mine
    owner = owner_of[...]

    def body(k, carry):
        pair = jnp.concatenate([table[2 * k], table[2 * k + 1]], axis=0)
        for i in range(BH):
            here = pl.ds(i * blocks, blocks)
            got = lax.dot_general(
                joined[here, :], pair, (((1,), (1,)), ((), ())), preferred_element_type=F32
            )
            new = jnp.where(owner == 2 * k, got[:, :128], acc[here, :])
            acc[here, :] = jnp.where(owner == 2 * k + 1, got[:, 128:], new)
        return carry

    acc[...] = jnp.zeros_like(acc)
    lax.fori_loop(0, table.shape[0] // 2, body, 0)
    fresh = []
    for i in range(BH):
        kept = kept_state[:, i * 128 : i * 128 + 128].astype(F32)
        value = kept + gelu(acc[i * blocks : (i + 1) * blocks, :])
        fresh.append(jnp.where(sea_of[...] > 0, value, 0.0).astype(BF16))
    sea_state[...] = jnp.dot(
        jnp.concatenate(fresh, axis=1), unspread[...], preferred_element_type=F32
    ).astype(BF16)


def call(kernel, out_shape, scratch, specs, limit):
    return pl.pallas_call(
        kernel,
        out_shape=out_shape,
        in_specs=[pl.BlockSpec(memory_space=s) for s in specs],
        out_specs=jax.tree.map(lambda _: pl.BlockSpec(memory_space=VMEM), out_shape),
        scratch_shapes=scratch,
        compiler_params=pltpu.CompilerParams(vmem_limit_bytes=limit * 2**20),
    )


def here(*xs):
    return [pltpu.with_memory_space_constraint(x, VMEM) for x in xs]


def local(
    atmosphere, ocean_state, land_sea, owners, rotations,
    conv_weight, conv_bias, force_weight, ocean_weight,
):
    tiles = lax.axis_size("tile")
    band_rows, columns, channels = atmosphere.shape
    blocks = owners.shape[0]
    shape = jax.ShapeDtypeStruct
    up_pairs = [(i, i + 1) for i in range(tiles - 1)]
    down_pairs = [(j, i) for i, j in up_pairs]
    padded = columns + 2 * PAD * SUB
    extended = band_rows + 2 * MARGIN
    field = pltpu.VMEM((band_rows, padded, channels), BF16)
    halo = pltpu.VMEM((MARGIN, columns, channels), BF16)
    middle = pltpu.VMEM((extended, padded, channels), BF16)
    paired = pltpu.VMEM((LAYERS, 1536, 256), BF16)
    results = pltpu.VMEM((2, GROUP * columns, 256), F32)

    own, send_up, send_down = call(
        rotate_kernel, (field, halo, halo), [], [SMEM, VMEM], 8
    )(rotations, atmosphere)
    up = lax.ppermute(send_up, "tile", up_pairs)
    down = lax.ppermute(send_down, "tile", down_pairs)

    packed = call(
        pack_kernel, pltpu.VMEM((tiles, 144, 128), BF16), [], [VMEM], 4
    )(jnp.swapaxes(ocean_weight[0], 1, 2).reshape(-1, 64))
    gathered = lax.all_to_all(here(packed)[0], "tile", 0, 0, tiled=True)

    weights = call(pair_weights, paired, [], [VMEM], 4)(conv_weight)

    lead_one, send_up, send_down = call(
        lead_one_kernel, (field, halo, halo), [middle, middle, results],
        [VMEM] * 5, 16,
    )(*here(own, up, down, weights), conv_bias)

    up = lax.ppermute(send_up, "tile", up_pairs)
    down = lax.ppermute(send_down, "tile", down_pairs)

    weights, *tables = call(
        table_kernel,
        (
            paired,
            pltpu.VMEM((tiles, 128, 768), BF16),
            pltpu.VMEM((blocks, 1024), BF16),
            pltpu.VMEM((blocks, 512), BF16),
            pltpu.VMEM((512, 512), BF16),
            pltpu.VMEM((blocks, 128), jnp.int32),
            pltpu.VMEM((blocks, 128), jnp.int32),
        ),
        [], [VMEM] * 5, 8,
    )(
        *here(gathered), conv_weight, ocean_state,
        owners.reshape(1, blocks), land_sea.reshape(1, blocks),
    )
    lead_one, up, down, weights, *tables = here(lead_one, up, down, weights, *tables)
    tops = call(
        early_kernel, (middle, middle), [results], [VMEM] * 4, 16
    )(lead_one, up, weights, conv_bias)

    return call(
        late_kernel,
        (shape(atmosphere.shape, BF16), shape(ocean_state.shape, BF16)),
        [
            middle, middle, results,
            pltpu.VMEM((band_rows, columns, channels), BF16),
            pltpu.VMEM((BH * blocks, 768), BF16),
            pltpu.VMEM((BH * blocks, 128), F32),
        ],
        [SMEM] + [VMEM] * 14, 20,
    )(
        rotations, lead_one, up, down, *here(*tops), weights, conv_bias, force_weight.T, *tables
    )


def solution(mesh):
    in_specs = (
        P(("ens", "tile"), None, None),
        P(("ens", "tile"), None),
        P("tile"),
        P("tile", None),
        P(),
        P(),
        P(),
        P(),
        P("tile", None, None, None),
    )
    out_specs = (P(("ens", "tile"), None, None), P(("ens", "tile"), None))

    return jax.shard_map(local, mesh=mesh, in_specs=in_specs, out_specs=out_specs, check_vma=False)
```

time: 72.8 us -> 66 us (0.907)
  the two profiles are of different devices: /device:TPU:19 before, /device:TPU:14 now
where the time goes in v2:
time: 66 us; the launch traced here: 65.6 us
  Pallas kernels  25 us (38%)
  waiting for transfers between devices  19.2 us (29%)
  starting transfers between devices  17.8 us (27%)
  local copies, waits for them, and re-layouts  2.69 us (4%)
  between operations  0.82 us (1%)
    ppermute x2, waiting for transfers between devices, local(): up = lax.ppermute(send_up, 'tile', up_pairs)  13.2 us
    pallas_call x1, Pallas kernels, local(): call(late_kernel, (shape(atmosphere.shape, BF16), shape(ocean_state.shape...  10.9 us
    ppermute x2, starting transfers between devices, local(): down = lax.ppermute(send_down, 'tile', down_pairs)  7.54 us
    pallas_call x1, Pallas kernels, local(): call(lead_one_kernel, (field, halo, halo), [middle, middle, results], [VM...  6.94 us
    all_to_all x1, starting transfers between devices, local(): gathered = lax.all_to_all(here(packed)[0], 'tile', 0, 0, tiled=True)  6.37 us
    ppermute x2, waiting for transfers between devices, local(): down = lax.ppermute(send_down, 'tile', down_pairs)  5.95 us
    ppermute x2, starting transfers between devices, local(): up = lax.ppermute(send_up, 'tile', up_pairs)  3.93 us
    pallas_call x1, Pallas kernels, local(): call(early_kernel, (middle, middle), [results], [VMEM] * 4, 16)  2.83 us
  transfers between devices with their start and end apart: 5, of which 3 were waited for; matrix products, arithmetic and copies ran while one was open for 0% of the time, Pallas kernels for 20%

profile of v2, /device:TPU:14, one launch (start us, length us, event | category | flops | bytes accessed | tf_op | source)
XLA Modules:
  0.0 65.6 jit_solution(16470656755512869443)
XLA Ops:
  0.6 0.0 copy-start
  0.6 0.0 copy-start.3
  0.6 1.0 %copy-done.3 = bf16[1,9,64,32]{2,3,1,0:T(8,128)(2,1)S(1)} copy-done((bf16[1,9,64,32]{2,3,1,0:T(8,128)(2,1)S(1)}, bf16[1,9,64,32]{2,3,1,0:T(8,128)(2,1)}, u32[]{:S(2)}) %copy-start.3) | copy-done | bytes 36888
  1.6 1.0 %shard_map.107 = bf16[16,144,128]{2,1,0:T(8,128)(2,1)} custom-call(bf16[288,64]{1,0:T(8,128)(2,1)S(1)} %bitcast.8), custom_call_target="tpu_custom_call" | custom-call | tf_op jit(solution)/shard_map/pallas_call | solution.py:416
  2.6 6.4 %all-to-all-start = ((bf16[16,144,128]{2,1,0:T(8,128)(2,1)}), bf16[16,144,128]{2,1,0:T(8,128)(2,1)S(1)}, u32[]{:S(2)}, u32[]{:S(2)}) async-start(bf16[16,144,128]{2,1,0:T(8,128)(2,1)} %shard_map.107), calls=%async_computation | async-start | bytes 1179648 | tf_op jit(solution)/shard_map/all_to_all | solution.py:419
  9.0 1.0 %copy-done.1 = bf16[8,256,128]{2,1,0:T(8,128)(2,1)S(1)} copy-done((bf16[8,256,128]{2,1,0:T(8,128)(2,1)S(1)}, bf16[8,256,128]{2,1,0:T(8,128)(2,1)}, u32[]{:S(2)}) %copy-start.1) | copy-done | bytes 524312
  10.0 0.7 copy-done.6
  10.7 0.9 %shard_map.104 = (bf16[8,384,128]{2,1,0:T(8,128)(2,1)S(1)}, bf16[7,256,128]{2,1,0:T(8,128)(2,1)S(1)}, bf16[7,256,128]{2,1,0:T(8,128)(2,1)S(1)}) custom-call(s32[16]{0:T(128)S(1)} %copy-done.6, bf16[8,256,128]{2,1,0:T(8,128)(2,1)S(1)} %copy-done.1), custom_call_target="tpu_custom_call" | custom-call | tf_op jit(solution)/shard_map/pallas_call | solution.py:410
  11.6 2.0 %collective-permute-start = (bf16[7,256,128]{2,1,0:T(8,128)(2,1)S(1)}, bf16[7,256,128]{2,1,0:T(8,128)(2,1)S(1)}, u32[]{:S(2)}, u32[]{:S(2)}) collective-permute-start(bf16[7,256,128]{2,1,0:T(8,128)(2,1)S(1)} %get-tuple-element.18), channel_id=1, source_target_pairs={{0,1},{1,2},{2,3},{3,4},{4,5},{5,6},{6,7},{7,8},{8,9},{9,10},{10,1... | collective-permute-start | bytes 1376264 | tf_op jit(solution)/shard_map/ppermute | solution.py:413
  13.6 3.5 %collective-permute-start.1 = (bf16[7,256,128]{2,1,0:T(8,128)(2,1)S(1)}, bf16[7,256,128]{2,1,0:T(8,128)(2,1)S(1)}, u32[]{:S(2)}, u32[]{:S(2)}) collective-permute-start(bf16[7,256,128]{2,1,0:T(8,128)(2,1)S(1)} %get-tuple-element.19), channel_id=1, source_target_pairs={{1,0},{2,1},{3,2},{4,3},{5,4},{6,5},{7,6},{8,7},{9,8},{10,9},{11,1... | collective-permute-start | bytes 1376264 | tf_op jit(solution)/shard_map/ppermute | solution.py:414
  17.1 0.0 copy-done
  17.2 0.3 shard_map.105.weights
  17.5 0.0 copy-start.2
  17.5 0.0 copy-start.8
  17.5 0.0 copy-start.9
  17.5 6.3 %collective-permute-done.up = bf16[7,256,128]{2,1,0:T(8,128)(2,1)S(1)} collective-permute-done((bf16[7,256,128]{2,1,0:T(8,128)(2,1)S(1)}, bf16[7,256,128]{2,1,0:T(8,128)(2,1)S(1)}, u32[]{:S(2)}, u32[]{:S(2)}) %collective-permute-start) | collective-permute-done | bytes 458784 | tf_op jit(solution)/shard_map/ppermute | solution.py:413
  23.8 6.0 %collective-permute-done.1.down = bf16[7,256,128]{2,1,0:T(8,128)(2,1)S(1)} collective-permute-done((bf16[7,256,128]{2,1,0:T(8,128)(2,1)S(1)}, bf16[7,256,128]{2,1,0:T(8,128)(2,1)S(1)}, u32[]{:S(2)}, u32[]{:S(2)}) %collective-permute-start.1) | collective-permute-done | bytes 458784 | tf_op jit(solution)/shard_map/ppermute | solution.py:414
  29.8 0.0 copy-done.4
  29.8 6.9 %shard_map.106 = (bf16[8,384,128]{2,1,0:T(8,128)(2,1)S(1)}, bf16[7,256,128]{2,1,0:T(8,128)(2,1)}, bf16[7,256,128]{2,1,0:T(8,128)(2,1)}) custom-call(bf16[8,384,128]{2,1,0:T(8,128)(2,1)S(1)} %get-tuple-element.17.own, bf16[7,256,128]{2,1,0:T(8,128)(2,1)S(1)} %collective-permute-done.up, bf16[7,256,128]{2,1,0:T(8,128)(2,1)S(1)} %collective-permute-done.1.down, ...), custom_call_target="tpu_custom_call" | custom-call | tf_op jit(solution)/shard_map/pallas_call | solution.py:423
  36.7 1.9 %collective-permute-start.2 = (bf16[7,256,128]{2,1,0:T(8,128)(2,1)}, bf16[7,256,128]{2,1,0:T(8,128)(2,1)S(1)}, u32[]{:S(2)}, u32[]{:S(2)}) collective-permute-start(bf16[7,256,128]{2,1,0:T(8,128)(2,1)} %get-tuple-element.21), channel_id=1, source_target_pairs={{0,1},{1,2},{2,3},{3,4},{4,5},{5,6},{6,7},{7,8},{8,9},{9,10},{10,1... | collective-permute-start | bytes 1376264 | tf_op jit(solution)/shard_map/ppermute | solution.py:428
  38.6 4.0 %collective-permute-start.3 = (bf16[7,256,128]{2,1,0:T(8,128)(2,1)}, bf16[7,256,128]{2,1,0:T(8,128)(2,1)S(1)}, u32[]{:S(2)}, u32[]{:S(2)}) collective-permute-start(bf16[7,256,128]{2,1,0:T(8,128)(2,1)} %get-tuple-element.22), channel_id=1, source_target_pairs={{1,0},{2,1},{3,2},{4,3},{5,4},{6,5},{7,6},{8,7},{9,8},{10,9},{11,1... | collective-permute-start | bytes 1376264 | tf_op jit(solution)/shard_map/ppermute | solution.py:429
  42.6 0.0 all-to-all-done.gathered
  42.7 0.0 copy-done.2
  42.7 0.0 copy-done.8
  42.7 0.0 copy-done.9
  42.7 0.0 copy-start.5
  42.7 0.0 copy-start.7
  42.7 2.2 %shard_map.108 = (bf16[3,1536,256]{2,1,0:T(8,128)(2,1)S(1)}, bf16[16,128,768]{2,1,0:T(8,128)(2,1)S(1)}, bf16[128,1024]{1,0:T(8,128)(2,1)S(1)}, bf16[128,512]{1,0...) custom-call(bf16[16,144,128]{2,1,0:T(8,128)(2,1)S(1)} %all-to-all-done.gathered, ...), custom_call_target="tpu_custom_call" | custom-call | tf_op jit(solution)/shard_map/pallas_call | solution.py:431
  44.9 6.9 %collective-permute-done.2.up = bf16[7,256,128]{2,1,0:T(8,128)(2,1)S(1)} collective-permute-done((bf16[7,256,128]{2,1,0:T(8,128)(2,1)}, bf16[7,256,128]{2,1,0:T(8,128)(2,1)S(1)}, u32[]{:S(2)}, u32[]{:S(2)}) %collective-permute-start.2) | collective-permute-done | bytes 458784 | tf_op jit(solution)/shard_map/ppermute | solution.py:428
  51.8 2.8 %shard_map.109 = (bf16[22,384,128]{2,1,0:T(8,128)(2,1)S(1)}, bf16[22,384,128]{2,1,0:T(8,128)(2,1)S(1)}) custom-call(bf16[8,384,128]{2,1,0:T(8,128)(2,1)S(1)} %get-tuple-element.20.own, bf16[7,256,128]{2,1,0:T(8,128)(2,1)S(1)} %collective-permute-done.2.up, bf16[3,1536,256]{2,1,0:T(8,128)(2,1)S(1)} %get-tuple-element.23.weights, bf16[3,128]{1,0:T(4,128)(2,1)S(1)} %copy-done.4), custom_call_target="tpu_custom_call" | custom-call | tf_op jit(solution)/shard_map/pallas_call | solution.py:448
  54.6 0.0 collective-permute-done.3.down
  54.7 10.9 %shard_map.110 = (bf16[8,256,128]{2,1,0:T(8,128)(2,1)}, bf16[128,512]{1,0:T(8,128)(2,1)}) custom-call(s32[16]{0:T(128)S(1)} %copy-done.7, bf16[8,384,128]{2,1,0:T(8,128)(2,1)S(1)} %get-tuple-element.20.own, bf16[7,256,128]{2,1,0:T(8,128)(2,1)S(1)} %collective-permute-done.2.up, bf16[7,256,128]{2,1,0:T(8,128)(2,1)S(1)} %collective-permute-done.3.down, ...), custom_call_target="tpu_custom_call" | custom-call | tf_op jit(solution)/shard_map/pallas_call | solution.py:452
  (5 shorter events, 0.0 us)
Async XLA Ops:
  0.6 16.5 %copy-start = (bf16[3,9,128,128]{3,2,1,0:T(8,128)(2,1)S(1)}, bf16[3,9,128,128]{3,2,1,0:T(8,128)(2,1)}, u32[]{:S(2)}) copy-start(bf16[3,9,128,128]{3,2,1,0:T(8,128)(2,1)} %conv_weight.3) | copy-start | bytes 2654212
  0.6 1.0 %copy-start.3 = (bf16[1,9,64,32]{2,3,1,0:T(8,128)(2,1)S(1)}, bf16[1,9,64,32]{2,3,1,0:T(8,128)(2,1)}, u32[]{:S(2)}) copy-start(bf16[1,9,64,32]{2,3,1,0:T(8,128)(2,1)} %param.17) | copy-start | bytes 110596
  2.6 27.2 %copy-start.4 = (bf16[3,128]{1,0:T(4,128)(2,1)S(1)}, bf16[3,128]{1,0:T(4,128)(2,1)}, u32[]{:S(2)}) copy-start(bf16[3,128]{1,0:T(4,128)(2,1)} %bias.5) | copy-start | bytes 2308
  2.6 40.0 %all-to-all-start = ((bf16[16,144,128]{2,1,0:T(8,128)(2,1)}), bf16[16,144,128]{2,1,0:T(8,128)(2,1)S(1)}, u32[]{:S(2)}, u32[]{:S(2)}) async-start(bf16[16,144,128]{2,1,0:T(8,128)(2,1)} %shard_map.107), calls=%async_computation | async-start | bytes 1179648 | tf_op jit(solution)/shard_map/all_to_all | solution.py:419
  9.0 1.0 %copy-start.1 = (bf16[8,256,128]{2,1,0:T(8,128)(2,1)S(1)}, bf16[8,256,128]{2,1,0:T(8,128)(2,1)}, u32[]{:S(2)}) copy-start(bf16[8,256,128]{2,1,0:T(8,128)(2,1)} %own.1) | copy-start | bytes 1572868
  10.0 0.7 copy-start.6
  11.6 12.3 %collective-permute-start = (bf16[7,256,128]{2,1,0:T(8,128)(2,1)S(1)}, bf16[7,256,128]{2,1,0:T(8,128)(2,1)S(1)}, u32[]{:S(2)}, u32[]{:S(2)}) collective-permute-start(bf16[7,256,128]{2,1,0:T(8,128)(2,1)S(1)} %get-tuple-element.18), channel_id=1, source_target_pairs={{0,1},{1,2},{2,3},{3,4},{4,5},{5,6},{6,7},{7,8},{8,9},{9,10},{10,1... | collective-permute-start | bytes 1376264 | tf_op jit(solution)/shard_map/ppermute | solution.py:413
  13.6 16.2 %collective-permute-start.1 = (bf16[7,256,128]{2,1,0:T(8,128)(2,1)S(1)}, bf16[7,256,128]{2,1,0:T(8,128)(2,1)S(1)}, u32[]{:S(2)}, u32[]{:S(2)}) collective-permute-start(bf16[7,256,128]{2,1,0:T(8,128)(2,1)S(1)} %get-tuple-element.19), channel_id=1, source_target_pairs={{1,0},{2,1},{3,2},{4,3},{5,4},{6,5},{7,6},{8,7},{9,8},{10,9},{11,1... | collective-permute-start | bytes 1376264 | tf_op jit(solution)/shard_map/ppermute | solution.py:414
  17.5 25.2 %copy-start.2 = (bf16[128,512]{1,0:T(8,128)(2,1)S(1)}, bf16[128,512]{1,0:T(8,128)(2,1)}, u32[]{:S(2)}) copy-start(bf16[128,512]{1,0:T(8,128)(2,1)} %state.1) | copy-start | bytes 393220
  17.5 25.2 %copy-start.8 = (s32[128,1]{0,1:T(1,128)S(1)}, s32[128,1]{0,1:T(1,128)}, u32[]{:S(2)}) copy-start(s32[128,1]{0,1:T(1,128)} %param.12) | copy-start | bytes 1540
  17.5 25.2 %copy-start.9 = (s32[128]{0:T(128)S(1)}, s32[128]{0:T(128)}, u32[]{:S(2)}) copy-start(s32[128]{0:T(128)} %param.11) | copy-start | bytes 1540
  36.7 15.1 %collective-permute-start.2 = (bf16[7,256,128]{2,1,0:T(8,128)(2,1)}, bf16[7,256,128]{2,1,0:T(8,128)(2,1)S(1)}, u32[]{:S(2)}, u32[]{:S(2)}) collective-permute-start(bf16[7,256,128]{2,1,0:T(8,128)(2,1)} %get-tuple-element.21), channel_id=1, source_target_pairs={{0,1},{1,2},{2,3},{3,4},{4,5},{5,6},{6,7},{7,8},{8,9},{9,10},{10,1... | collective-permute-start | bytes 1376264 | tf_op jit(solution)/shard_map/ppermute | solution.py:428
  38.6 16.0 %collective-permute-start.3 = (bf16[7,256,128]{2,1,0:T(8,128)(2,1)}, bf16[7,256,128]{2,1,0:T(8,128)(2,1)S(1)}, u32[]{:S(2)}, u32[]{:S(2)}) collective-permute-start(bf16[7,256,128]{2,1,0:T(8,128)(2,1)} %get-tuple-element.22), channel_id=1, source_target_pairs={{1,0},{2,1},{3,2},{4,3},{5,4},{6,5},{7,6},{8,7},{9,8},{10,9},{11,1... | collective-permute-start | bytes 1376264 | tf_op jit(solution)/shard_map/ppermute | solution.py:429
  42.7 12.0 %copy-start.5 = (bf16[128,32]{0,1:T(8,128)(2,1)S(1)}, bf16[128,32]{0,1:T(8,128)(2,1)}, u32[]{:S(2)}) copy-start(bf16[128,32]{0,1:T(8,128)(2,1)} %param.16) | copy-start | bytes 24580
  42.7 12.0 %copy-start.7 = (s32[16]{0:T(128)S(1)}, s32[16]{0:T(128)}, u32[]{:S(2)}) copy-start(s32[16]{0:T(128)} %rotations.3) | copy-start | bytes 196

commit v3 on v2

v3 whole, which is shorter than its diff:
```python
import jax
import jax.numpy as jnp
from jax import lax
from jax.experimental import pallas as pl
from jax.experimental.pallas import tpu as pltpu
from jax.sharding import PartitionSpec as P


LAYERS = 3
BH = 4
BW = 4
SUB = 16
PAD = 4
GROUP = 2
MARGIN = 2**LAYERS - 1
F32 = jnp.float32
BF16 = jnp.bfloat16
VMEM = pltpu.MemorySpace.VMEM
SMEM = pltpu.MemorySpace.SMEM


def gelu(x):
    half = 0.5 * x
    inner = x * (0.7978845608028654 + 0.035677408136300125 * (x * x))
    return half + half * jnp.tanh(inner)


def one_hot_columns(columns, shift, source_permuted, target_permuted):
    target = lax.broadcasted_iota(jnp.int32, (columns, columns), 0)
    source = lax.broadcasted_iota(jnp.int32, (columns, columns), 1)
    tiles = columns // SUB
    if target_permuted:
        target = (target % SUB) * tiles + target // SUB
    if source_permuted:
        source = (source % SUB) * tiles + source // SUB
    wanted = (target + shift) & (columns - 1)
    return jnp.where(wanted == source, 1.0, 0.0).astype(BF16)


def store_row(ref, row, value, reach):
    columns = value.shape[0]
    ref[row, PAD * SUB : PAD * SUB + columns, :] = value.astype(BF16)
    for k in range(reach):
        first = value[k * SUB : (k + 1) * SUB]
        at = PAD * SUB + columns + k * SUB
        ref[row, at : at + SUB, :] = pltpu.roll(first, SUB - 1, 0).astype(BF16)
        low = columns - (k + 1) * SUB
        last = value[low : low + SUB]
        at = PAD * SUB - (k + 1) * SUB
        ref[row, at : at + SUB, :] = pltpu.roll(last, 1, 0).astype(BF16)


def layer_rows(layer, band_rows):
    used = 2 ** (layer + 1) - 1
    return list(range(used, band_rows + 2 * MARGIN - used))


def row_groups(rows, dilation, size):
    rows = set(rows)
    firsts = []
    while rows:
        r = min(rows)
        firsts.append(r)
        rows -= {r, r + dilation}
    return [firsts[k : k + size] for k in range(0, len(firsts), size)]


def flipped():
    return lax.axis_index("tile") % 2 == 0


def far_tile():
    tile = lax.axis_index("tile")
    return tile + jnp.where(tile % 2 == 0, -1, 1)


def turn(index, count):
    return jnp.where(flipped(), count - 1 - index, index)


def give_row(row, value, field, send_near, send_far):
    store_row(field, row, value, 1)
    if row < MARGIN:
        send_near[MARGIN - 1 - row] = value.astype(BF16)
    if row > 0:
        send_far[MARGIN - row] = value.astype(BF16)


def rotate_kernel(
    rotations, atmosphere, field, send_near, send_far, own, shifts, own_sem, shift_sem
):
    get_shifts = pltpu.make_async_copy(rotations, shifts, shift_sem)
    get_own = pltpu.make_async_copy(atmosphere, own, own_sem)
    get_shifts.start()
    get_own.start()
    band_rows, columns = own.shape[0], own.shape[1]
    get_shifts.wait()
    hot = one_hot_columns(columns, -shifts[lax.axis_index("tile")], False, True)
    get_own.wait()
    for k in range(0, band_rows, 2):
        pair = [own[turn(k + half, band_rows)] for half in range(2)]
        moved = jnp.dot(hot, jnp.concatenate(pair, axis=1), preferred_element_type=F32)
        for half in range(2):
            give_row(k + half, moved[:, half * 128 : half * 128 + 128], field, send_near, send_far)


def pack_kernel(ocean_weight, packed):
    taps = ocean_weight[...].astype(F32)
    none = jnp.zeros((32, 32), F32)
    for tap_row in range(3):
        for half in range(2):
            cells = [
                taps[(tap_row * 3 + b) * 32 : (tap_row * 3 + b) * 32 + 32, half * 32 : half * 32 + 32]
                for b in range(3)
            ]
            at = (tap_row * 2 + half) * 32
            packed[0, at : at + 32, :] = jnp.concatenate(cells + [none], axis=1).astype(BF16)


def pair_weights(conv_weight, weights):
    zero = jnp.zeros((384, 128), BF16)
    for layer in range(LAYERS):
        for half in range(2):
            at = (1 - half) * 1152
            weights[layer, at : at + 384, half * 128 : half * 128 + 128] = zero
            for tap_row in range(3):
                for tap in range(3):
                    at = half * 384 + tap_row * 384 + tap * 128
                    weights[layer, at : at + 128, half * 128 : half * 128 + 128] = conv_weight[
                        layer, turn(tap_row, 3) * 3 + tap
                    ]


def conv_rows(plan, place, sink, weights, bias, results, band_rows, columns):
    reach = far_tile()
    inside = (reach >= 0) & (reach < lax.axis_size("tile"))
    inside = jnp.where(inside, 1.0, 0.0).astype(F32)

    def piece(ref, row, moved):
        padded = ref.shape[1] > columns
        if padded or moved == 0:
            start = (PAD * SUB if padded else 0) + moved * SUB
            return ref[row, start : start + columns, :]
        edge = ref[row, columns - SUB :, :] if moved < 0 else ref[row, :SUB, :]
        edge = pltpu.roll(edge.astype(F32), 1 if moved < 0 else SUB - 1, 0).astype(BF16)
        if moved < 0:
            return jnp.concatenate([edge, ref[row, : columns - SUB, :]], axis=0)
        return jnp.concatenate([ref[row, SUB:, :], edge], axis=0)

    def product(layer, group, out):
        dilation = 2**layer
        stacked = []
        for first in group:
            pieces = []
            for rho in range(4):
                ref, row = place(layer, first + (rho - 1) * dilation)
                for tap in range(3):
                    pieces.append(piece(ref, row, (tap - 1) * dilation))
            stacked.append(jnp.concatenate(pieces, axis=1))
        out[: len(group) * columns, :] = jnp.dot(
            jnp.concatenate(stacked, axis=0), weights[layer], preferred_element_type=F32
        )

    def finish(layer, group, got):
        offset = bias[layer][None, :].astype(F32)
        for k, first in enumerate(group):
            for half in range(2):
                at = first + half * 2**layer
                ref, row = place(layer, at)
                kept = piece(ref, row, 0).astype(F32)
                summed = got[k * columns : (k + 1) * columns, half * 128 : half * 128 + 128]
                value = kept + gelu(summed + offset)
                if layer + 1 == LAYERS:
                    sink(at, value)
                    continue
                if at >= MARGIN + band_rows:
                    value = value * inside
                ref, row = place(layer + 1, at)
                store_row(ref, row, value, 2 ** (layer + 1))

    for k, (layer, group) in enumerate(plan):
        if k and plan[k - 1][0] == layer:
            product(layer, group, results.at[k % 2])
            finish(*plan[k - 1], results.at[(k - 1) % 2])
        else:
            if k:
                finish(*plan[k - 1], results.at[(k - 1) % 2])
            product(layer, group, results.at[k % 2])
    finish(*plan[-1], results.at[(len(plan) - 1) % 2])


def plans(band_rows):
    edge = MARGIN + band_rows
    ready = edge - 1
    early, late = [], []
    for layer in range(LAYERS):
        dilation = 2**layer
        rows = layer_rows(layer, band_rows)
        ready -= dilation
        first = [r for r in rows if r <= ready]
        first = first[: len(first) // (2 * dilation) * 2 * dilation]
        ready = first[-1] if first else 0
        early += [(layer, g) for g in row_groups(first, dilation, GROUP)]
        rest = [r for r in rows if r not in first]
        late += [(layer, g) for g in row_groups(rest, dilation, GROUP)]
    return early, late


def pick(own, near, far, e):
    band_rows = own.shape[0]
    if e < MARGIN:
        return near, e
    if e < MARGIN + band_rows:
        return own, e - MARGIN
    return far, e - MARGIN - band_rows


def early_kernel(own, near, weights, bias, top_a, top_b, results):
    band_rows, columns = own.shape[0], near.shape[1]

    def place(layer, e):
        if layer == 0:
            return pick(own, near, None, e)
        return (top_a, top_b)[layer - 1], e

    conv_rows(plans(band_rows)[0], place, None, weights, bias, results, band_rows, columns)


def late_rows(own, near, far, top_a, top_b, weights, bias, mid_a, mid_b, results, sink):
    band_rows, columns = own.shape[0], near.shape[1]
    early, late = plans(band_rows)
    firsts = [
        {r for l, g in early for f in g for r in (f, f + 2**l) if l == layer}
        for layer in range(LAYERS)
    ]

    def place(layer, e):
        if layer == 0:
            return pick(own, near, far, e)
        if e in firsts[layer - 1]:
            return (top_a, top_b)[layer - 1], e
        return (mid_a, mid_b)[layer - 1], e

    conv_rows(late, place, sink, weights, bias, results, band_rows, columns)


def late_one_kernel(
    own, near, far, top_a, top_b, weights, bias, field, send_near, send_far, *scratch
):
    def sink(e, value):
        give_row(e - MARGIN, value, field, send_near, send_far)

    late_rows(own, near, far, top_a, top_b, weights, bias, *scratch, sink)


def by_owner(joined, table, owner_of, acc):
    tiles = table.shape[0]
    blocks = owner_of.shape[0]
    bits = tiles.bit_length() - 1
    tile = lax.axis_index("tile")

    def owner_at(slot):
        mirrored = sum(((slot >> k) & 1) << (bits - 1 - k) for k in range(bits))
        return tile ^ mirrored

    def body(k, carry):
        pair = jnp.concatenate([table[2 * k], table[2 * k + 1]], axis=0)
        got = lax.dot_general(
            joined[...], pair, (((1,), (1,)), ((), ())), preferred_element_type=F32
        )
        first = owner_of[...] == owner_at(2 * k)
        second = owner_of[...] == owner_at(2 * k + 1)
        for i in range(BH):
            rows = slice(i * blocks, i * blocks + blocks)
            new = jnp.where(first, got[rows, :128], acc[rows, :])
            acc[rows, :] = jnp.where(second, got[rows, 128:], new)
        return carry

    acc[...] = jnp.zeros_like(acc)
    lax.fori_loop(0, tiles // 2, body, 0, unroll=tiles <= 16)


def table_kernel(*refs):
    *pieces, state, owners, sea = refs[:-8]
    table, kept_state, unspread, owner_of, sea_of, acc, joined, state_table = refs[-8:]
    blocks = state.shape[0]
    owner_of[...] = jnp.transpose(jnp.broadcast_to(owners[...], (128, blocks)))
    sea_of[...] = jnp.transpose(jnp.broadcast_to(sea[...], (128, blocks)))

    a = lax.broadcasted_iota(jnp.int32, (512, 512), 0)
    b = lax.broadcasted_iota(jnp.int32, (512, 512), 1)
    unspread[...] = jnp.where(a == ((b & 15) << 5) + (b >> 4), 1.0, 0.0).astype(BF16)
    spread = jnp.where(((b & 31) << 4) + (b >> 5) == a, 1.0, 0.0).astype(BF16)
    kept = jnp.dot(state[...], spread, preferred_element_type=F32).astype(BF16)
    kept_state[...] = kept
    none = jnp.zeros((blocks, 128), BF16)
    for i in range(BH):
        for tap_row in range(3):
            at = i + tap_row - 1
            joined[i * blocks : (i + 1) * blocks, tap_row * 128 : tap_row * 128 + 128] = (
                kept[:, at * 128 : at * 128 + 128] if 0 <= at < BH else none
            )

    lane = lax.broadcasted_iota(jnp.int32, (32, 128), 1)
    base = 0
    for piece in pieces:

        def body(k, carry, piece=piece, base=base):
            for tap_row in range(3):
                for half, to in enumerate((table, state_table)):
                    at = (tap_row * 2 + half) * 32
                    strip = piece[k, at : at + 32, :].astype(F32)
                    for j in range(BW):
                        moved = strip if j == 1 else pltpu.roll(strip, 32 * (j - 1) % 128, 1)
                        if j == 0:
                            moved = jnp.where(lane < 96, moved, 0.0)
                        if j == 3:
                            moved = jnp.where(lane >= 32, moved, 0.0)
                        to[base + k, j * 32 : j * 32 + 32, tap_row * 128 : tap_row * 128 + 128] = (
                            moved.astype(BF16)
                        )
            return carry

        lax.fori_loop(0, piece.shape[0], body, 0)
        base += piece.shape[0]
    by_owner(joined, state_table, owner_of, acc)


def late_two_kernel(
    rotations, own, near, far, top_a, top_b, weights, bias, force,
    table, kept_state, unspread, owner_of, sea_of, state_part,
    atmos_out, sea_state, mid_a, mid_b, results, last, joined, acc,
):
    band_rows, columns = own.shape[0], near.shape[1]

    def sink(e, value):
        last[e - MARGIN] = value.astype(BF16)

    late_rows(own, near, far, top_a, top_b, weights, bias, mid_a, mid_b, results, sink)

    shift = rotations[lax.axis_index("tile")]
    repeated = jnp.concatenate([force[...]] * BW, axis=0)
    repeated = jnp.concatenate([repeated, repeated], axis=1)
    per_half = columns // BW
    cells = lax.broadcasted_iota(jnp.int32, (columns, columns), 0)
    stored = lax.broadcasted_iota(jnp.int32, (columns, columns), 1)
    wanted = ((cells % per_half) * BW + cells // per_half + shift) & (columns - 1)
    gather = jnp.where(
        wanted == (stored % SUB) * (columns // SUB) + stored // SUB, 1.0, 0.0
    ).astype(BF16)
    lane = lax.broadcasted_iota(jnp.int32, (per_half, 256), 1) % 128 // 32
    blocks = band_rows // BH * per_half
    joined[...] = jnp.zeros_like(joined)
    for row in range(0, band_rows, 2):
        forcing = []
        for k in range(2):
            at = turn(row + k, band_rows)
            both = jnp.concatenate(
                [own[at, PAD * SUB : PAD * SUB + columns, :], last[at]], axis=1
            )
            summed = lax.dot_general(
                both, repeated, (((1,), (1,)), ((), ())), preferred_element_type=F32
            )
            forcing.append((0.5 * summed).astype(BF16))
        spots = jnp.dot(gather, jnp.concatenate(forcing, axis=1), preferred_element_type=F32)
        mine = spots[:per_half]
        for q in range(1, BW):
            mine = jnp.where(lane == q, spots[q * per_half : (q + 1) * per_half], mine)
        mine = mine.astype(BF16)
        first = row // BH * per_half
        for k in range(2):
            for tap_row in range(3):
                to = row % BH + k - tap_row + 1
                if 0 <= to < BH:
                    joined[
                        to * blocks + first : to * blocks + first + per_half,
                        tap_row * 128 : tap_row * 128 + 128,
                    ] = mine[:, k * 128 : k * 128 + 128]
    by_owner(joined, table, owner_of, acc)

    hot = one_hot_columns(columns, shift, True, False)
    for row in range(0, band_rows, 2):
        pair = [last[turn(row + half, band_rows)] for half in range(2)]
        moved = jnp.dot(hot, jnp.concatenate(pair, axis=1), preferred_element_type=F32)
        atmos_out[row] = moved[:, :128].astype(BF16)
        atmos_out[row + 1] = moved[:, 128:].astype(BF16)

    fresh = []
    for i in range(BH):
        rows = slice(i * blocks, i * blocks + blocks)
        kept = kept_state[:, i * 128 : i * 128 + 128].astype(F32)
        value = kept + gelu(acc[rows, :] + state_part[rows, :])
        fresh.append(jnp.where(sea_of[...] > 0, value, 0.0).astype(BF16))
    sea_state[...] = jnp.dot(
        jnp.concatenate(fresh, axis=1), unspread[...], preferred_element_type=F32
    ).astype(BF16)


def call(kernel, out_shape, scratch, specs, limit):
    return pl.pallas_call(
        kernel,
        out_shape=out_shape,
        in_specs=[pl.BlockSpec(memory_space=s) for s in specs],
        out_specs=jax.tree.map(lambda _: pl.BlockSpec(memory_space=VMEM), out_shape),
        scratch_shapes=scratch,
        compiler_params=pltpu.CompilerParams(vmem_limit_bytes=limit * 2**20),
    )


def here(*xs):
    return [pltpu.with_memory_space_constraint(x, VMEM) for x in xs]


def exchange(send_near, send_far, tiles):
    far_pairs = [(t, t + 1 if t % 2 else t - 1) for t in range(1, tiles - 1)]
    far = lax.ppermute(send_far, "tile", far_pairs)
    near = lax.ppermute(send_near, "tile", [(t, t ^ 1) for t in range(tiles)])
    return here(near, far)


def local(
    atmosphere, ocean_state, land_sea, owners, rotations,
    conv_weight, conv_bias, force_weight, ocean_weight,
):
    tiles = lax.axis_size("tile")
    band_rows, columns, channels = atmosphere.shape
    blocks = owners.shape[0]
    shape = jax.ShapeDtypeStruct
    padded = columns + 2 * PAD * SUB
    extended = band_rows + 2 * MARGIN
    field = pltpu.VMEM((band_rows, padded, channels), BF16)
    halo = pltpu.VMEM((MARGIN, columns, channels), BF16)
    middle = pltpu.VMEM((extended, padded, channels), BF16)
    results = pltpu.VMEM((2, GROUP * columns, 256), F32)

    own, send_near, send_far = call(
        rotate_kernel, (field, halo, halo),
        [
            pltpu.VMEM(atmosphere.shape, BF16),
            pltpu.SMEM(rotations.shape, jnp.int32),
            pltpu.SemaphoreType.DMA,
            pltpu.SemaphoreType.DMA,
        ],
        [pl.ANY, pl.ANY], 8,
    )(rotations, atmosphere)
    near, far = exchange(send_near, send_far, tiles)

    pieces = [
        call(pack_kernel, pltpu.VMEM((1, 192, 128), BF16), [], [VMEM], 4)(
            jnp.swapaxes(ocean_weight[0], 1, 2).reshape(-1, 64)
        )
    ]
    have = pieces[0]
    step = tiles // 2
    while step:
        pieces.append(lax.ppermute(have, "tile", [(t, t ^ step) for t in range(tiles)]))
        if step > 1:
            have = jnp.concatenate([have, pieces[-1]], axis=0)
        step //= 2

    weights = call(pair_weights, pltpu.VMEM((LAYERS, 1536, 256), BF16), [], [VMEM], 4)(conv_weight)
    own, weights = here(own, weights)

    def early(own, near):
        return here(
            *call(early_kernel, (middle, middle), [results], [VMEM] * 4, 16)(
                own, near, weights, conv_bias
            )
        )

    tops = early(own, near)
    own, send_near, send_far = call(
        late_one_kernel, (field, halo, halo), [middle, middle, results],
        [VMEM] * 7, 16,
    )(own, near, far, *tops, weights, conv_bias)
    (own,) = here(own)
    near, far = exchange(send_near, send_far, tiles)
    tops = early(own, near)

    tables = call(
        table_kernel,
        (
            pltpu.VMEM((tiles, 128, 384), BF16),
            pltpu.VMEM((blocks, 512), BF16),
            pltpu.VMEM((512, 512), BF16),
            pltpu.VMEM((blocks, 128), jnp.int32),
            pltpu.VMEM((blocks, 128), jnp.int32),
            pltpu.VMEM((BH * blocks, 128), F32),
        ),
        [pltpu.VMEM((BH * blocks, 384), BF16), pltpu.VMEM((tiles, 128, 384), BF16)],
        [VMEM] * (len(pieces) + 3), 8 + tiles // 4,
    )(*here(*pieces), ocean_state, owners.reshape(1, blocks), land_sea.reshape(1, blocks))

    return call(
        late_two_kernel,
        (shape(atmosphere.shape, BF16), shape(ocean_state.shape, BF16)),
        [
            middle, middle, results,
            pltpu.VMEM((band_rows, columns, channels), BF16),
            pltpu.VMEM((BH * blocks, 384), BF16),
            pltpu.VMEM((BH * blocks, 128), F32),
        ],
        [SMEM] + [VMEM] * 14, 20,
    )(
        rotations, own, near, far, *tops, weights, conv_bias, force_weight.T, *here(*tables)
    )


def solution(mesh):
    in_specs = (
        P(("ens", "tile"), None, None),
        P(("ens", "tile"), None),
        P("tile"),
        P("tile", None),
        P(),
        P(),
        P(),
        P(),
        P("tile", None, None, None),
    )
    out_specs = (P(("ens", "tile"), None, None), P(("ens", "tile"), None))

    return jax.shard_map(local, mesh=mesh, in_specs=in_specs, out_specs=out_specs, check_vma=False)
```

time: 66 us -> 51 us (0.77)
  the two profiles are of different devices: /device:TPU:14 before, /device:TPU:1 now
where the time goes in v3:
time: 51 us; the launch traced here: 50.7 us
  Pallas kernels  20.6 us (40%)
  starting transfers between devices  18.5 us (36%)
  waiting for transfers between devices  6.94 us (14%)
  local copies, waits for them, and re-layouts  3.78 us (7%)
  between operations  0.82 us (2%)
    ppermute x4, starting transfers between devices, local(): lax.ppermute(have, 'tile', [(t, t ^ step) for t in range(tiles)])  9.13 us
    pallas_call x1, Pallas kernels, local(): call(late_two_kernel, (shape(atmosphere.shape, BF16), shape(ocean_state.s...  7.15 us
    ppermute x2, starting transfers between devices, exchange(): far = lax.ppermute(send_far, 'tile', far_pairs)  6.76 us
    pallas_call x2, Pallas kernels, early(): call(early_kernel, (middle, middle), [results], [VMEM] * 4, 16)  5.59 us
    ppermute x4, waiting for transfers between devices, local(): lax.ppermute(have, 'tile', [(t, t ^ step) for t in range(tiles)])  4.68 us
    unnamed x20, local copies, waits for them, and re-layouts  3.78 us
    pallas_call x1, Pallas kernels, local(): call(late_one_kernel, (field, halo, halo), [middle, middle, results], [VM...  3.36 us
    pallas_call x1, Pallas kernels, local(): call(table_kernel, (pltpu.VMEM((tiles, 128, 384), BF16), pltpu.VMEM((bloc...  3.18 us
  transfers between devices with their start and end apart: 8, of which 3 were waited for; matrix products, arithmetic and copies ran while one was open for 0% of the time, Pallas kernels for 26%

profile of v3, /device:TPU:1, one launch (start us, length us, event | category | flops | bytes accessed | tf_op | source)
XLA Modules:
  0.0 50.7 jit_solution(5824545695745019263)
XLA Ops:
  0.6 0.9 %copy-done.3 = bf16[1,9,64,32]{2,3,1,0:T(8,128)(2,1)S(1)} copy-done((bf16[1,9,64,32]{2,3,1,0:T(8,128)(2,1)S(1)}, bf16[1,9,64,32]{2,3,1,0:T(8,128)(2,1)}, u32[]{:S(2)}) %copy-start.3) | copy-done | bytes 36888
  1.5 0.1 shard_map.109.refs_0_
  1.6 3.2 %collective-permute-start.4 = (bf16[1,192,128]{2,1,0:T(8,128)(2,1)S(1)}, bf16[1,192,128]{2,1,0:T(8,128)(2,1)S(1)}, u32[]{:S(2)}, u32[]{:S(2)}) collective-permute-start(bf16[1,192,128]{2,1,0:T(8,128)(2,1)S(1)} %shard_map.109.refs_0_), channel_id=1, source_target_pairs={{0,8},{1,9},{2,10},{3,11},{4,12},{5,13},{6,14},{7,15},{8,0},{9,1},... | collective-permute-start | bytes 147464 | tf_op jit(solution)/shard_map/ppermute | solution.py:456
  4.8 1.0 %copy-done.1 = bf16[8,256,128]{2,1,0:T(8,128)(2,1)S(1)} copy-done((bf16[8,256,128]{2,1,0:T(8,128)(2,1)S(1)}, bf16[8,256,128]{2,1,0:T(8,128)(2,1)}, u32[]{:S(2)}) %copy-start.1) | copy-done | bytes 524312
  5.9 0.7 %copy-done.6 = s32[16]{0:T(128)S(1)} copy-done((s32[16]{0:T(128)S(1)}, s32[16]{0:T(128)}, u32[]{:S(2)}) %copy-start.6) | copy-done | bytes 88
  6.5 1.0 %shard_map.104 = (bf16[8,384,128]{2,1,0:T(8,128)(2,1)S(1)}, bf16[7,256,128]{2,1,0:T(8,128)(2,1)S(1)}, bf16[7,256,128]{2,1,0:T(8,128)(2,1)S(1)}) custom-call(s32[16]{0:T(128)S(1)} %copy-done.6, bf16[8,256,128]{2,1,0:T(8,128)(2,1)S(1)} %copy-done.1), custom_call_target="tpu_custom_call" | custom-call | tf_op jit(solution)/shard_map/pallas_call | solution.py:436
  7.5 1.0 %collective-permute-start = (bf16[7,256,128]{2,1,0:T(8,128)(2,1)S(1)}, bf16[7,256,128]{2,1,0:T(8,128)(2,1)S(1)}, u32[]{:S(2)}, u32[]{:S(2)}) collective-permute-start(bf16[7,256,128]{2,1,0:T(8,128)(2,1)S(1)} %get-tuple-element.19), channel_id=1, source_target_pairs={{0,1},{1,0},{2,3},{3,2},{4,5},{5,4},{6,7},{7,6},{8,9},{9,8},{10,11... | collective-permute-start | bytes 1376264 | tf_op jit(solution)/shard_map/ppermute | solution.py:417
  8.5 3.0 %collective-permute-start.1 = (bf16[7,256,128]{2,1,0:T(8,128)(2,1)S(1)}, bf16[7,256,128]{2,1,0:T(8,128)(2,1)S(1)}, u32[]{:S(2)}, u32[]{:S(2)}) collective-permute-start(bf16[7,256,128]{2,1,0:T(8,128)(2,1)S(1)} %get-tuple-element.20), channel_id=1, source_target_pairs={{1,2},{2,1},{3,4},{4,3},{5,6},{6,5},{7,8},{8,7},{9,10},{10,9},{11,... | collective-permute-start | bytes 1376264 | tf_op jit(solution)/shard_map/ppermute | solution.py:416
  11.6 0.0 collective-permute-done.4.refs_1_
  11.6 1.4 %collective-permute-start.5 = (bf16[2,192,128]{2,1,0:T(8,128)(2,1)S(1)}, bf16[2,192,128]{2,1,0:T(8,128)(2,1)S(1)}, u32[]{:S(2)}, u32[]{:S(2)}) collective-permute-start(bf16[2,192,128]{2,1,0:T(8,128)(2,1)S(1)} %pad_maximum_fusion.2), channel_id=1, source_target_pairs={{0,4},{1,5},{2,6},{3,7},{4,0},{5,1},{6,2},{7,3},{8,12},{9,13},{10,... | collective-permute-start | bytes 294920 | tf_op jit(solution)/shard_map/ppermute | solution.py:456
  13.0 3.0 %collective-permute-done.5.refs_2_ = bf16[2,192,128]{2,1,0:T(8,128)(2,1)S(1)} collective-permute-done((bf16[2,192,128]{2,1,0:T(8,128)(2,1)S(1)}, bf16[2,192,128]{2,1,0:T(8,128)(2,1)S(1)}, u32[]{:S(2)}, u32[]{:S(2)}) %collective-permute-start.5) | collective-permute-done | bytes 98336 | tf_op jit(solution)/shard_map/ppermute | solution.py:456
  15.9 4.5 %collective-permute-start.6 = (bf16[4,192,128]{2,1,0:T(8,128)(2,1)S(1)}, bf16[4,192,128]{2,1,0:T(8,128)(2,1)S(1)}, u32[]{:S(2)}, u32[]{:S(2)}) collective-permute-start(bf16[4,192,128]{2,1,0:T(8,128)(2,1)S(1)} %pad_maximum_fusion.1), channel_id=1, source_target_pairs={{0,2},{1,3},{2,0},{3,1},{4,6},{5,7},{6,4},{7,5},{8,10},{9,11},{10,... | collective-permute-start | bytes 589832 | tf_op jit(solution)/shard_map/ppermute | solution.py:456
  20.4 1.2 %copy-done = bf16[3,9,128,128]{3,2,1,0:T(8,128)(2,1)S(1)} copy-done((bf16[3,9,128,128]{3,2,1,0:T(8,128)(2,1)S(1)}, bf16[3,9,128,128]{3,2,1,0:T(8,128)(2,1)}, u32[]{:S(2)}) %copy-start) | copy-done | bytes 884760
  21.6 0.3 shard_map.105.weights
  21.9 0.0 collective-permute-done.near
  21.9 2.8 %shard_map.106 = (bf16[22,384,128]{2,1,0:T(8,128)(2,1)S(1)}, bf16[22,384,128]{2,1,0:T(8,128)(2,1)S(1)}) custom-call(bf16[8,384,128]{2,1,0:T(8,128)(2,1)S(1)} %get-tuple-element.18.own, bf16[7,256,128]{2,1,0:T(8,128)(2,1)S(1)} %collective-permute-done.near, bf16[3,1536,256]{2,1,0:T(8,128)(2,1)S(1)} %shard_map.105.weights, bf16[3,128]{1,0:T(4,128)(2,1)S(1)} %copy-done.4), custom_call_target="tpu_custom_call" | custom-call | tf_op jit(solution)/shard_map/pallas_call | solution.py:466
  24.7 0.0 collective-permute-done.1.far
  24.7 0.0 copy-start.2
  24.8 0.0 copy-start.8
  24.8 0.0 copy-start.9
  24.8 3.4 %shard_map.107 = (bf16[8,384,128]{2,1,0:T(8,128)(2,1)S(1)}, bf16[7,256,128]{2,1,0:T(8,128)(2,1)S(1)}, bf16[7,256,128]{2,1,0:T(8,128)(2,1)S(1)}) custom-call(bf16[8,384,128]{2,1,0:T(8,128)(2,1)S(1)} %get-tuple-element.18.own, bf16[7,256,128]{2,1,0:T(8,128)(2,1)S(1)} %collective-permute-done.near, bf16[7,256,128]{2,1,0:T(8,128)(2,1)S(1)} %collective-permute-done.1.far, ...), custom_call_target="tpu_custom_call" | custom-call | tf_op jit(solution)/shard_map/pallas_call | solution.py:472
  28.1 1.6 %collective-permute-start.2 = (bf16[7,256,128]{2,1,0:T(8,128)(2,1)S(1)}, bf16[7,256,128]{2,1,0:T(8,128)(2,1)S(1)}, u32[]{:S(2)}, u32[]{:S(2)}) collective-permute-start(bf16[7,256,128]{2,1,0:T(8,128)(2,1)S(1)} %get-tuple-element.24), channel_id=1, source_target_pairs={{0,1},{1,0},{2,3},{3,2},{4,5},{5,4},{6,7},{7,6},{8,9},{9,8},{10,11... | collective-permute-start | bytes 1376264 | tf_op jit(solution)/shard_map/ppermute | solution.py:417
  29.7 3.7 %collective-permute-start.3 = (bf16[7,256,128]{2,1,0:T(8,128)(2,1)S(1)}, bf16[7,256,128]{2,1,0:T(8,128)(2,1)S(1)}, u32[]{:S(2)}, u32[]{:S(2)}) collective-permute-start(bf16[7,256,128]{2,1,0:T(8,128)(2,1)S(1)} %get-tuple-element.25), channel_id=1, source_target_pairs={{1,2},{2,1},{3,4},{4,3},{5,6},{6,5},{7,8},{8,7},{9,10},{10,9},{11,... | collective-permute-start | bytes 1376264 | tf_op jit(solution)/shard_map/ppermute | solution.py:416
  33.4 0.0 collective-permute-done.6.refs_3_
  33.5 0.1 collective-permute-start.7
  33.6 1.7 %collective-permute-done.7.refs_4_ = bf16[8,192,128]{2,1,0:T(8,128)(2,1)S(1)} collective-permute-done((bf16[8,192,128]{2,1,0:T(8,128)(2,1)S(1)}, bf16[8,192,128]{2,1,0:T(8,128)(2,1)S(1)}, u32[]{:S(2)}, u32[]{:S(2)}) %collective-permute-start.7) | collective-permute-done | bytes 393248 | tf_op jit(solution)/shard_map/ppermute | solution.py:456
  35.3 0.0 copy-start.5
  35.3 0.0 copy-start.7
  35.3 3.2 %shard_map.110 = (bf16[16,128,384]{2,1,0:T(8,128)(2,1)S(1)}, bf16[128,512]{1,0:T(8,128)(2,1)S(1)}, bf16[512,512]{1,0:T(8,128)(2,1)S(1)}, s32[128,128]{1,0:T(8,12...) custom-call(bf16[1,192,128]{2,1,0:T(8,128)(2,1)S(1)} %shard_map.109.refs_0_, ...), custom_call_target="tpu_custom_call" | custom-call | tf_op jit(solution)/shard_map/pallas_call | solution.py:480
  38.5 2.8 %shard_map.108 = (bf16[22,384,128]{2,1,0:T(8,128)(2,1)S(1)}, bf16[22,384,128]{2,1,0:T(8,128)(2,1)S(1)}) custom-call(bf16[8,384,128]{2,1,0:T(8,128)(2,1)S(1)} %get-tuple-element.23.own, bf16[7,256,128]{2,1,0:T(8,128)(2,1)S(1)} %collective-permute-done.2.near, bf16[3,1536,256]{2,1,0:T(8,128)(2,1)S(1)} %shard_map.105.weights, bf16[3,128]{1,0:T(4,128)(2,1)S(1)} %copy-done.4), custom_call_target="tpu_custom_call" | custom-call | tf_op jit(solution)/shard_map/pallas_call | solution.py:466
  41.3 2.3 %collective-permute-done.3.far = bf16[7,256,128]{2,1,0:T(8,128)(2,1)S(1)} collective-permute-done((bf16[7,256,128]{2,1,0:T(8,128)(2,1)S(1)}, bf16[7,256,128]{2,1,0:T(8,128)(2,1)S(1)}, u32[]{:S(2)}, u32[]{:S(2)}) %collective-permute-start.3) | collective-permute-done | bytes 458784 | tf_op jit(solution)/shard_map/ppermute | solution.py:416
  43.6 7.2 %shard_map.111 = (bf16[8,256,128]{2,1,0:T(8,128)(2,1)}, bf16[128,512]{1,0:T(8,128)(2,1)}) custom-call(s32[16]{0:T(128)S(1)} %copy-done.7, bf16[8,384,128]{2,1,0:T(8,128)(2,1)S(1)} %get-tuple-element.23.own, bf16[7,256,128]{2,1,0:T(8,128)(2,1)S(1)} %collective-permute-done.2.near, bf16[7,256,128]{2,1,0:T(8,128)(2,1)S(1)} %collective-permute-done.3.far, ...), custom_call_target="tpu_custom_call" | custom-call | tf_op jit(solution)/shard_map/pallas_call | solution.py:494
  (15 shorter events, 0.1 us)
Async XLA Ops:
  0.6 0.9 %copy-start.3 = (bf16[1,9,64,32]{2,3,1,0:T(8,128)(2,1)S(1)}, bf16[1,9,64,32]{2,3,1,0:T(8,128)(2,1)}, u32[]{:S(2)}) copy-start(bf16[1,9,64,32]{2,3,1,0:T(8,128)(2,1)} %param.17) | copy-start | bytes 110596
  1.6 9.9 %collective-permute-start.4 = (bf16[1,192,128]{2,1,0:T(8,128)(2,1)S(1)}, bf16[1,192,128]{2,1,0:T(8,128)(2,1)S(1)}, u32[]{:S(2)}, u32[]{:S(2)}) collective-permute-start(bf16[1,192,128]{2,1,0:T(8,128)(2,1)S(1)} %shard_map.109.refs_0_), channel_id=1, source_target_pairs={{0,8},{1,9},{2,10},{3,11},{4,12},{5,13},{6,14},{7,15},{8,0},{9,1},... | collective-permute-start | bytes 147464 | tf_op jit(solution)/shard_map/ppermute | solution.py:456
  4.8 1.0 %copy-start.1 = (bf16[8,256,128]{2,1,0:T(8,128)(2,1)S(1)}, bf16[8,256,128]{2,1,0:T(8,128)(2,1)}, u32[]{:S(2)}) copy-start(bf16[8,256,128]{2,1,0:T(8,128)(2,1)} %atmosphere.1) | copy-start | bytes 1572868
  5.9 0.7 %copy-start.6 = (s32[16]{0:T(128)S(1)}, s32[16]{0:T(128)}, u32[]{:S(2)}) copy-start(s32[16]{0:T(128)} %rotations.3) | copy-start | bytes 196
  6.5 15.4 %copy-start.4 = (bf16[3,128]{1,0:T(4,128)(2,1)S(1)}, bf16[3,128]{1,0:T(4,128)(2,1)}, u32[]{:S(2)}) copy-start(bf16[3,128]{1,0:T(4,128)(2,1)} %bias.7) | copy-start | bytes 2308
  7.5 14.4 %collective-permute-start = (bf16[7,256,128]{2,1,0:T(8,128)(2,1)S(1)}, bf16[7,256,128]{2,1,0:T(8,128)(2,1)S(1)}, u32[]{:S(2)}, u32[]{:S(2)}) collective-permute-start(bf16[7,256,128]{2,1,0:T(8,128)(2,1)S(1)} %get-tuple-element.19), channel_id=1, source_target_pairs={{0,1},{1,0},{2,3},{3,2},{4,5},{5,4},{6,7},{7,6},{8,9},{9,8},{10,11... | collective-permute-start | bytes 1376264 | tf_op jit(solution)/shard_map/ppermute | solution.py:417
  8.5 16.2 %collective-permute-start.1 = (bf16[7,256,128]{2,1,0:T(8,128)(2,1)S(1)}, bf16[7,256,128]{2,1,0:T(8,128)(2,1)S(1)}, u32[]{:S(2)}, u32[]{:S(2)}) collective-permute-start(bf16[7,256,128]{2,1,0:T(8,128)(2,1)S(1)} %get-tuple-element.20), channel_id=1, source_target_pairs={{1,2},{2,1},{3,4},{4,3},{5,6},{6,5},{7,8},{8,7},{9,10},{10,9},{11,... | collective-permute-start | bytes 1376264 | tf_op jit(solution)/shard_map/ppermute | solution.py:416
  11.6 4.3 %collective-permute-start.5 = (bf16[2,192,128]{2,1,0:T(8,128)(2,1)S(1)}, bf16[2,192,128]{2,1,0:T(8,128)(2,1)S(1)}, u32[]{:S(2)}, u32[]{:S(2)}) collective-permute-start(bf16[2,192,128]{2,1,0:T(8,128)(2,1)S(1)} %pad_maximum_fusion.2), channel_id=1, source_target_pairs={{0,4},{1,5},{2,6},{3,7},{4,0},{5,1},{6,2},{7,3},{8,12},{9,13},{10,... | collective-permute-start | bytes 294920 | tf_op jit(solution)/shard_map/ppermute | solution.py:456
  15.9 17.5 %collective-permute-start.6 = (bf16[4,192,128]{2,1,0:T(8,128)(2,1)S(1)}, bf16[4,192,128]{2,1,0:T(8,128)(2,1)S(1)}, u32[]{:S(2)}, u32[]{:S(2)}) collective-permute-start(bf16[4,192,128]{2,1,0:T(8,128)(2,1)S(1)} %pad_maximum_fusion.1), channel_id=1, source_target_pairs={{0,2},{1,3},{2,0},{3,1},{4,6},{5,7},{6,4},{7,5},{8,10},{9,11},{10,... | collective-permute-start | bytes 589832 | tf_op jit(solution)/shard_map/ppermute | solution.py:456
  20.4 1.2 %copy-start = (bf16[3,9,128,128]{3,2,1,0:T(8,128)(2,1)S(1)}, bf16[3,9,128,128]{3,2,1,0:T(8,128)(2,1)}, u32[]{:S(2)}) copy-start(bf16[3,9,128,128]{3,2,1,0:T(8,128)(2,1)} %conv_weight.1) | copy-start | bytes 2654212
  24.7 10.5 %copy-start.2 = (bf16[128,512]{1,0:T(8,128)(2,1)S(1)}, bf16[128,512]{1,0:T(8,128)(2,1)}, u32[]{:S(2)}) copy-start(bf16[128,512]{1,0:T(8,128)(2,1)} %refs_5_.1) | copy-start | bytes 393220
  24.8 10.5 %copy-start.8 = (s32[128,1]{0,1:T(1,128)S(1)}, s32[128,1]{0,1:T(1,128)}, u32[]{:S(2)}) copy-start(s32[128,1]{0,1:T(1,128)} %param.12) | copy-start | bytes 1540
  24.8 10.5 %copy-start.9 = (s32[128]{0:T(128)S(1)}, s32[128]{0:T(128)}, u32[]{:S(2)}) copy-start(s32[128]{0:T(128)} %param.11) | copy-start | bytes 1540
  28.1 10.4 %collective-permute-start.2 = (bf16[7,256,128]{2,1,0:T(8,128)(2,1)S(1)}, bf16[7,256,128]{2,1,0:T(8,128)(2,1)S(1)}, u32[]{:S(2)}, u32[]{:S(2)}) collective-permute-start(bf16[7,256,128]{2,1,0:T(8,128)(2,1)S(1)} %get-tuple-element.24), channel_id=1, source_target_pairs={{0,1},{1,0},{2,3},{3,2},{4,5},{5,4},{6,7},{7,6},{8,9},{9,8},{10,11... | collective-permute-start | bytes 1376264 | tf_op jit(solution)/shard_map/ppermute | solution.py:417
  29.7 13.9 %collective-permute-start.3 = (bf16[7,256,128]{2,1,0:T(8,128)(2,1)S(1)}, bf16[7,256,128]{2,1,0:T(8,128)(2,1)S(1)}, u32[]{:S(2)}, u32[]{:S(2)}) collective-permute-start(bf16[7,256,128]{2,1,0:T(8,128)(2,1)S(1)} %get-tuple-element.25), channel_id=1, source_target_pairs={{1,2},{2,1},{3,4},{4,3},{5,6},{6,5},{7,8},{8,7},{9,10},{10,9},{11,... | collective-permute-start | bytes 1376264 | tf_op jit(solution)/shard_map/ppermute | solution.py:416
  33.5 1.8 %collective-permute-start.7 = (bf16[8,192,128]{2,1,0:T(8,128)(2,1)S(1)}, bf16[8,192,128]{2,1,0:T(8,128)(2,1)S(1)}, u32[]{:S(2)}, u32[]{:S(2)}) collective-permute-start(bf16[8,192,128]{2,1,0:T(8,128)(2,1)S(1)} %pad_maximum_fusion), channel_id=1, source_target_pairs={{0,1},{1,0},{2,3},{3,2},{4,5},{5,4},{6,7},{7,6},{8,9},{9,8},{10,11... | collective-permute-start | bytes 1179656 | tf_op jit(solution)/shard_map/ppermute | solution.py:456
  35.3 8.3 %copy-start.5 = (bf16[128,32]{0,1:T(8,128)(2,1)S(1)}, bf16[128,32]{0,1:T(8,128)(2,1)}, u32[]{:S(2)}) copy-start(bf16[128,32]{0,1:T(8,128)(2,1)} %param.16) | copy-start | bytes 24580
  35.3 8.3 %copy-start.7 = (s32[16]{0:T(128)S(1)}, s32[16]{0:T(128)}, u32[]{:S(2)}) copy-start(s32[16]{0:T(128)} %rotations.3) | copy-start | bytes 196
